TPU v7x, 32 devices: a whole 2x2x4 slice. The times are simulated.
32 devices in a mesh: role: 2 (over y), tile: 16 (over z, x, core).
Axes of the slice: x: 2, y: 2, z: 4, core: 2. Of those that a mesh axis runs over, the one named last changes fastest.
Arguments:
- fields_pair: float32 [2, 512, 16384], P('role', None, 'tile'), may hold values from 0 to 1
- velocity: float32 [16384], P('tile'), may hold values from -0.5 to 0.5
- growth: float32 [16384], P('tile'), may hold values from 0.05 to 0.5
- features: bfloat16 [512, 1024], replicated, may hold values from -6 to 6
- assignment: int32 [512], replicated, may hold values from 0 to 511, each once
- out_pair: float32 [2, 1024, 16384], P('role', None, 'tile'), may hold values from -0.1875 to 0.1875
- hidden_pair: float32 [2, 5, 1024, 1024], P('role', None, 'tile'), may hold values from -0.1875 to 0.1875
Outputs:
- fields_next: float32 [2, 512, 16384], P('role', None, 'tile')
- out_next: float32 [2, 1024, 16384], P('role', None, 'tile')
- hidden_next: float32 [2, 5, 1024, 1024], P('role', None, 'tile')
Inputs may be any that keep to these rules, and one draw needn't show every extreme that they name: `assignment`: a permutation of the 512 members.
All inputs are finite; a program needn't handle non-finite values.
Results may differ from a plain program's by a relative error of at most 0.0022.
The roundings to bfloat16 on the way count: a program that leaves them out, or rounds other values in their place, can miss the bound.
Values may be sent and summed in bfloat16 or wider, within the bound.
A program may use at most 192 MiB of HBM per device.

v0:
```python
import jax
import jax.numpy as jnp
from jax import lax
from jax.sharding import PartitionSpec as P

BATCH = 512


momentum_decay = 0.9
step_size = 0.1


def extended(value, sides, width):
    for axis, dim in sides:
        count, length = (lax.axis_size(axis), value.shape[dim])
        up = [(i, (i + 1) % count) for i in range(count)]
        down = [(j, i) for i, j in up]
        last = lax.slice_in_dim(value, length - width, length, axis=dim)
        leading = lax.slice_in_dim(value, 0, width, axis=dim)
        before = lax.ppermute(last, axis, up)
        after = lax.ppermute(leading, axis, down)
        value = jnp.concatenate([before, value, after], axis=dim)
    return value


def spread(block, axis, owner):
    block = jnp.where(lax.axis_index(axis) == owner, block, jnp.zeros_like(block))
    return lax.psum(block, axis)


def partner(value, axis, distance):
    return lax.ppermute(value, axis, [(i, i ^ 1 << distance) for i in range(lax.axis_size(axis))])


def guarded(flag, action, *operands):

    def skipped(*values):
        return jax.tree.map(jnp.zeros_like, action(*values))

    return lax.cond(flag, action, skipped, *operands)


def silu_slope(values):
    logistic = jax.nn.sigmoid(values)
    return logistic * (1.0 + values * (1.0 - logistic))


def advance(padded, growth):
    states = padded[:-1]
    velocity_row = padded[-1]
    outflow = (
        jnp.maximum(velocity_row[:-1], 0.0) * states[:, :-1]
        + jnp.minimum(velocity_row[:-1], 0.0) * states[:, 1:]
    )
    carried = states[:, 1:-1] - outflow[:, 1:] + outflow[:, :-1]
    return carried + growth * carried * (1.0 - carried)


def body(fields_pair, velocity, growth, features, assignment, out_pair, hidden_pair):
    solver_side = lax.axis_index("role") == 0
    trainer_side = jnp.logical_not(solver_side)
    own_fields = fields_pair[0]
    own_out = out_pair[0]
    own_hidden = hidden_pair[0]
    layer_count = own_hidden.shape[0]
    unit_rows = own_hidden.shape[1]
    first_unit = lax.axis_index("tile") * unit_rows
    stacked = jnp.concatenate([own_fields, velocity[None, :]], axis=0)
    padded = extended(stacked, (("tile", 1),), 1)
    advanced = guarded(solver_side, advance, padded, growth)
    fresh_fields = spread(advanced, "role", 0)
    out_narrow = own_out.astype(jnp.bfloat16)
    hidden_narrow = own_hidden.astype(jnp.bfloat16)
    full_hidden = lax.all_gather(hidden_narrow, "tile", axis=1, tiled=True)

    def forward(features, full_hidden, out_narrow, target):
        inputs = []
        summed_list = []
        activation = features
        for layer_index in range(layer_count):
            inputs.append(activation)
            summed = jnp.dot(
                activation, full_hidden[layer_index], preferred_element_type=jnp.float32
            )
            summed_list.append(summed)
            activation = jax.nn.silu(summed).astype(jnp.bfloat16)
        predicted = jnp.dot(activation, out_narrow, preferred_element_type=jnp.float32)
        residual = ((predicted - target) / BATCH).astype(jnp.bfloat16)
        grad_out = jnp.dot(activation.T, residual, preferred_element_type=jnp.float32)
        partial_grad = lax.dot_general(
            residual, out_narrow, (((1,), (1,)), ((), ())), preferred_element_type=jnp.float32
        )
        return (jnp.stack(summed_list), jnp.stack(inputs), grad_out, partial_grad)

    summed_all, inputs_all, grad_out, partial_grad = guarded(
        trainer_side, forward, features, full_hidden, out_narrow, own_fields
    )
    upstream = lax.psum(partial_grad, "tile")

    def backward(summed_all, inputs_all, upstream, full_hidden, first_unit):
        gradients = []
        for layer_index in reversed(range(layer_count)):
            slope = (upstream * silu_slope(summed_all[layer_index])).astype(jnp.bfloat16)
            own_inputs = lax.dynamic_slice_in_dim(inputs_all[layer_index], first_unit, unit_rows, 1)
            gradients.append(jnp.dot(own_inputs.T, slope, preferred_element_type=jnp.float32))
            if layer_index > 0:
                upstream = lax.dot_general(
                    slope,
                    full_hidden[layer_index],
                    (((1,), (1,)), ((), ())),
                    preferred_element_type=jnp.float32,
                )
        return jnp.stack(gradients[::-1])

    grad_hidden = guarded(
        trainer_side, backward, summed_all, inputs_all, upstream, full_hidden, first_unit
    )
    solver_pack = jnp.concatenate([own_out.reshape(-1), own_hidden.reshape(-1)])
    trainer_pack = jnp.concatenate([grad_out.reshape(-1), grad_hidden.reshape(-1)])
    payload = jnp.where(solver_side, solver_pack, trainer_pack)
    received = partner(payload, "role", 0)
    out_length = own_out.size
    other_out = received[:out_length].reshape(own_out.shape)
    other_hidden = received[out_length:].reshape(own_hidden.shape)
    out_next = jnp.where(
        solver_side,
        momentum_decay * own_out + other_out,
        own_out - step_size * (momentum_decay * other_out + grad_out),
    )
    hidden_next = jnp.where(
        solver_side,
        momentum_decay * own_hidden + other_hidden,
        own_hidden - step_size * (momentum_decay * other_hidden + grad_hidden),
    )
    fields_next = jnp.where(solver_side, advanced, jnp.take(fresh_fields, assignment, axis=0))
    return (fields_next[None], out_next[None], hidden_next[None])


def solution(mesh):
    return jax.shard_map(
        body,
        mesh=mesh,
        in_specs=(
            P("role", None, "tile"),
            P("tile"),
            P("tile"),
            P(),
            P(),
            P("role", None, "tile"),
            P("role", None, "tile", None),
        ),
        out_specs=(P("role", None, "tile"), P("role", None, "tile"), P("role", None, "tile", None)),
        check_vma=False,
    )
```

profile of v0, /device:TPU:0, one launch (start us, length us, event | category | flops | bytes accessed | tf_op | source)
XLA Modules:
  0.0 473.0 jit_solution(12022284242264037515)
XLA Ops:
  8.1 2.4 bitcast_convert_fusion
  10.5 91.3 %all-gather.2.cloned.1.call-done = bf16[5,1024,1024]{2,1,0:T(8,128)(2,1)} async-done(((bf16[5,64,1024]{2,1,0:T(8,128)(2,1)}), bf16[5,1024,1024]{2,1,0:T(8,128)(2,1)}) %all-gather.2.cloned.1.call-update) | async-done | bytes 10485776 | tf_op jit(solution)/shard_map/all_gather | solution.py:74
  101.9 14.5 %conditional.4 = (f32[5,512,1024]{2,1,0:T(8,128)}, bf16[5,512,1024]{2,1,0:T(8,128)(2,1)}, f32[1024,1024]{1,0:T(8,128)}, f32[512,1024]{1,0:T(8,128)}, f32[1048576]{0:T(1024)}) conditional(s32[]{:T(128)} %convert_element_type.53, () %tuple.39, (bf16[5,1024,1024]{2,1,0:T(8,128)(2,1)}, bf16[512,1024]{1,0:T(8,128)(2,1)}, f32[1024,1024]{1,0:T(8,128)}, ...), branch_computations={%region_3.4_spmd, %region_4.5_spmd} | conditional | flops 8619819008 | bytes 140509344 | solution.py:40
  101.9 5.2 %broadcast.47 = f32[5,512,1024]{2,1,0:T(8,128)} broadcast(f32[]{:T(128)} %constant.41.clone), dimensions={} | broadcast | bytes 10485764 | tf_op jit(solution)/shard_map/broadcast.16
  107.1 3.0 broadcast.48
  110.1 2.5 broadcast.49
  112.6 2.2 reshape.52
  114.8 1.6 broadcast.50
  116.5 5.4 %copy.14 = f32[128,8,8,128]{3,1,2,0:T(8,128)} copy(f32[128,8,8,128]{3,2,1,0:T(8,128)} %bitcast.240) | data formatting | bytes 8388608
  122.2 113.0 %all-reduce.5.cloned.1.call-done = f32[512,1024]{1,0:T(8,128)} async-done(((f32[512,1024]{1,0:T(8,128)}), f32[512,1024]{1,0:T(8,128)}) %all-reduce.5.cloned.1.call-update) | async-done | bytes 2097168 | tf_op jit(solution)/shard_map/psum | solution.py:98
  235.2 2.4 conditional.5
  235.2 1.2 broadcast.52
  236.4 1.1 reshape.54
  237.5 6.3 %maximum_select_fusion = f32[1376256]{0:T(1024)} fusion(f32[327680]{0:T(1024)S(1)} %bitcast.246, f32[1048576]{0:T(1024)} %bitcast.241, f32[327680]{0:T(1024)} %get-tuple-element.66, f32[1048576]{0:T(1024)} %get-tuple-element.62, pred[]{:T(512)S(6)} %eq.4), kind=kLoop, calls=%fused_computation.125 | loop fusion | flops 4128768 | bytes 16515073 | tf_op jit(solution)/shard_map/jit(_where)/select_n | solution.py:120
  243.9 37.5 %collective-permute-start.2 = (f32[1376256]{0:T(1024)}, f32[1376256]{0:T(1024)}, u32[]{:S(2)}, u32[]{:S(2)}) collective-permute-start(f32[1376256]{0:T(1024)} %maximum_select_fusion), channel_id=1, source_target_pairs={{0,16},{16,0},{1,17},{17,1},{2,18},{18,2},{3,19},{19,3},{4,20},{20... | collective-permute-start | bytes 16515080 | tf_op jit(solution)/shard_map/ppermute | solution.py:32
  281.6 4.4 collective-permute-start.1
  286.0 1.6 pad_maximum_fusion
  287.6 2.6 collective-permute-done
  290.2 3.1 concatenate.13
  293.3 3.4 conditional.3
  293.6 0.7 multiply_add_fusion
  294.3 2.5 multiply_add_fusion.1
  296.8 3.2 broadcast_select_fusion
  300.7 107.6 %all-reduce.3.cloned.1.call-done = f32[512,1024]{1,0:T(8,128)} async-done(((f32[512,1024]{1,0:T(8,128)}), f32[512,1024]{1,0:T(8,128)}) %all-reduce.3.cloned.1.call-update) | async-done | bytes 2097168 | tf_op jit(solution)/shard_map/psum | solution.py:28
  408.2 4.4 gather_fusion
  412.6 3.2 select_bitcast_fusion.1
  415.8 28.6 %collective-permute-done.2 = f32[1376256]{0:T(1024)} collective-permute-done((f32[1376256]{0:T(1024)}, f32[1376256]{0:T(1024)}, u32[]{:S(2)}, u32[]{:S(2)}) %collective-permute-start.2) | collective-permute-done | bytes 5505056 | tf_op jit(solution)/shard_map/ppermute | solution.py:32
  444.4 1.4 slice.144
  446.1 4.4 slice.143
  450.5 5.1 %slice.132 = f32[1024,1024]{1,0:T(8,128)} reshape(f32[1048576]{0:T(1024)} %slice.143) | data formatting | bytes 8388608 | tf_op jit(solution)/shard_map/slice | solution.py:123
  455.6 3.0 fusion.100
  458.6 7.1 %select_bitcast_fusion = f32[1,1024,1024]{2,1,0:T(8,128)} fusion(f32[1024,1024]{1,0:T(8,128)} %get-tuple-element.67, f32[1024,1024]{1,0:T(8,128)} %slice.132, pred[]{:T(512)S(6)} %eq.4, f32[1,1024,1024]{2,1,0:T(8,128)S(1)} %copy-done), kind=kLoop, calls=%fused_computation.126 | loop fusion | flops 7340032 | bytes 16777216 | tf_op jit(solution)/shard_map/broadcast_in_dim | solution.py:136
  (29 shorter events, 1.6 us)
Async XLA Ops:
  8.0 93.9 %copy-start.4 = (f32[1,512,1024]{2,1,0:T(8,128)S(1)}, f32[1,512,1024]{2,1,0:T(8,128)}, u32[]{:S(2)}) copy-start(f32[1,512,1024]{2,1,0:T(8,128)} %param.13) | copy-start | bytes 6291460
  8.0 93.9 %all-gather.2.cloned.1.call-start = ((), (), s32[]{:S(2)}) async-start(), calls=%async_computation.1 | async-start | bytes 11141120 | tf_op jit(solution)/shard_map/all_gather | solution.py:74
  10.5 224.7 %all-reduce.5.cloned.1.call-start = ((), (), s32[]{:S(2)}) async-start(), calls=%async_computation.2 | async-start | bytes 4194304 | tf_op jit(solution)/shard_map/psum | solution.py:98
  116.4 291.8 %all-reduce.3.cloned.1.call-start = ((), (), s32[]{:S(2)}) async-start(), calls=%async_computation | async-start | bytes 4194304 | tf_op jit(solution)/shard_map/psum | solution.py:28
  116.5 5.4 %copy-start.2 = (f32[1,5,64,1024]{3,2,1,0:T(8,128)S(1)}, f32[1,5,64,1024]{3,2,1,0:T(8,128)}, u32[]{:S(2)}) copy-start(f32[1,5,64,1024]{3,2,1,0:T(8,128)} %param.19) | copy-start | bytes 3932164
  237.5 43.8 %copy-start.11 = (f32[1024]{0:T(1024)S(1)}, f32[1024]{0:T(1024)}, u32[]{:S(2)}) copy-start(f32[1024]{0:T(1024)} %param.14) | copy-start | bytes 12292
  243.9 200.6 %collective-permute-start.2 = (f32[1376256]{0:T(1024)}, f32[1376256]{0:T(1024)}, u32[]{:S(2)}, u32[]{:S(2)}) collective-permute-start(f32[1376256]{0:T(1024)} %maximum_select_fusion), channel_id=1, source_target_pairs={{0,16},{16,0},{1,17},{17,1},{2,18},{18,2},{3,19},{19,3},{4,20},{20... | collective-permute-start | bytes 16515080 | tf_op jit(solution)/shard_map/ppermute | solution.py:32
  281.5 8.7 %collective-permute-start = (f32[513,1]{1,0:T(8,128)S(1)}, f32[513,1]{1,0:T(8,128)S(1)}, u32[]{:S(2)}, u32[]{:S(2)}) collective-permute-start(f32[513,1]{1,0:T(8,128)S(1)} %get-tuple-element.91), channel_id=1, source_target_pairs={{0,1},{1,2},{2,3},{3,4},{4,5},{5,6},{6,7},{7,8},{8,9},{9,10},{10,1... | collective-permute-start | bytes 6164 | tf_op jit(solution)/shard_map/ppermute | solution.py:20
  281.6 8.6 %collective-permute-start.1 = (f32[513,1]{1,0:T(8,128)S(1)}, f32[513,1]{1,0:T(8,128)S(1)}, u32[]{:S(2)}, u32[]{:S(2)}) collective-permute-start(f32[513,1]{1,0:T(8,128)S(1)} %get-tuple-element.90), channel_id=1, source_target_pairs={{1,0},{2,1},{3,2},{4,3},{5,4},{6,5},{7,6},{8,7},{9,8},{10,9},{11,1... | collective-permute-start | bytes 6164 | tf_op jit(solution)/shard_map/ppermute | solution.py:21
  287.6 5.7 %copy-start.13 = (f32[1024]{0:T(1024)S(1)}, f32[1024]{0:T(1024)}, u32[]{:S(2)}) copy-start(f32[1024]{0:T(1024)} %param.15) | copy-start | bytes 12292
  300.0 0.7 copy-start.12
  450.5 5.1 %copy-start.3 = (f32[1,5,64,1024]{3,2,1,0:T(8,128)S(1)}, f32[1,5,64,1024]{3,2,1,0:T(8,128)}, u32[]{:S(2)}) copy-start(f32[1,5,64,1024]{3,2,1,0:T(8,128)} %param.19) | copy-start | bytes 3932164
  455.6 3.0 copy-start
Sparse Core Ops, SparseCore 0:
  11.6 90.2 all-gather.1
  116.6 118.5 all-reduce.4
Sparse Core Ops, SparseCore 1:
  300.1 108.1 all-reduce.2
where the time goes:
time: 473 us
  waiting for transfers between devices  343 us (73%)
  starting transfers between devices  42.1 us (9%)
  local copies, waits for them, and re-layouts  41.8 us (9%)
  other arithmetic  30.1 us (6%)
  between operations  15.6 us (3%)
    psum x1, waiting for transfers between devices, body(): upstream = lax.psum(partial_grad, 'tile')  113 us
    psum x1, waiting for transfers between devices, spread(): return lax.psum(block, axis)  108 us
    all_gather x1, waiting for transfers between devices, body(): full_hidden = lax.all_gather(hidden_narrow, 'tile', axis=1, tiled=True)  91.3 us
    ppermute x1, starting transfers between devices, partner(): lax.ppermute(value, axis, [(i, i ^ 1 << distance) for i in range(lax.axis...  37.5 us
    ppermute x1, waiting for transfers between devices, partner(): lax.ppermute(value, axis, [(i, i ^ 1 << distance) for i in range(lax.axis...  28.6 us
    another operation x5, local copies, waits for them, and re-layouts  13.6 us
    broadcast_in_dim x3, other arithmetic, body(): return (fields_next[None], out_next[None], hidden_next[None])  13.2 us
    slice x2, local copies, waits for them, and re-layouts, body(): other_out = received[:out_length].reshape(own_out.shape)  9.5 us
  transfers between devices with their start and end apart: 6, of which 5 were waited for; matrix products, arithmetic and copies ran while one was open for 5% of the time, Pallas kernels for 0%

commit v1 on v0

v1 whole, which is shorter than its diff:
```python
import jax
import jax.numpy as jnp
from jax import lax
from jax.sharding import PartitionSpec as P

momentum_decay = 0.9
step_size = 0.1


def extended(value, axis, dim, width):
    count, length = (lax.axis_size(axis), value.shape[dim])
    up = [(i, (i + 1) % count) for i in range(count)]
    down = [(j, i) for i, j in up]
    last = lax.slice_in_dim(value, length - width, length, axis=dim)
    leading = lax.slice_in_dim(value, 0, width, axis=dim)
    before = lax.ppermute(last, axis, up)
    after = lax.ppermute(leading, axis, down)
    return jnp.concatenate([before, value, after], axis=dim)


def silu_slope(values):
    logistic = jax.nn.sigmoid(values)
    return logistic * (1.0 + values * (1.0 - logistic))


def advance(padded, growth):
    states = padded[:-1]
    velocity_row = padded[-1]
    outflow = (
        jnp.maximum(velocity_row[:-1], 0.0) * states[:, :-1]
        + jnp.minimum(velocity_row[:-1], 0.0) * states[:, 1:]
    )
    carried = states[:, 1:-1] - outflow[:, 1:] + outflow[:, :-1]
    return carried + growth * carried * (1.0 - carried)


def to_trainer(value):
    return lax.ppermute(value.astype(jnp.bfloat16), "role", [(0, 1)])


def to_solver(value):
    return lax.ppermute(value.astype(jnp.bfloat16), "role", [(1, 0)])


def plain_training(features, hidden_narrow, out_narrow, own_fields, own_out, own_hidden):
    layer_count, unit_rows = own_hidden.shape[:2]
    batch = own_fields.shape[0]
    first_unit = lax.axis_index("tile") * unit_rows
    momentum_out = to_trainer(own_out)
    momentum_hidden = to_trainer(own_hidden)
    full_hidden = [
        lax.all_gather(hidden_narrow[i], "tile", axis=0, tiled=True) for i in range(layer_count)
    ]
    inputs, summed_list = [], []
    activation = features
    for i in range(layer_count):
        inputs.append(activation)
        summed = jnp.dot(activation, full_hidden[i], preferred_element_type=jnp.float32)
        summed_list.append(summed)
        activation = jax.nn.silu(summed).astype(jnp.bfloat16)
    predicted = jnp.dot(activation, out_narrow, preferred_element_type=jnp.float32)
    residual = ((predicted - own_fields) / batch).astype(jnp.bfloat16)
    partial_grad = lax.dot_general(
        residual, out_narrow, (((1,), (1,)), ((), ())), preferred_element_type=jnp.float32
    )
    upstream = lax.psum(partial_grad, "tile")
    grad_out = jnp.dot(activation.T, residual, preferred_element_type=jnp.float32)
    sent_out = to_solver(grad_out)
    gradients, sent = [], []
    for i in reversed(range(layer_count)):
        slope = (upstream * silu_slope(summed_list[i])).astype(jnp.bfloat16)
        own_inputs = lax.dynamic_slice_in_dim(inputs[i], first_unit, unit_rows, 1)
        gradient = jnp.dot(own_inputs.T, slope, preferred_element_type=jnp.float32)
        gradients.append(gradient)
        sent.append(to_solver(gradient))
        if i > 0:
            upstream = lax.dot_general(
                slope, full_hidden[i], (((1,), (1,)), ((), ())), preferred_element_type=jnp.float32
            )
    solver_side = lax.axis_index("role") == 0
    other_out = jnp.where(solver_side, sent_out, momentum_out)
    other_hidden = jnp.where(solver_side, jnp.stack(sent[::-1]), momentum_hidden)
    return grad_out, jnp.stack(gradients[::-1]), other_out, other_hidden


def body(fields_pair, velocity, growth, features, assignment, out_pair, hidden_pair):
    solver_side = lax.axis_index("role") == 0
    own_fields = fields_pair[0]
    own_out = out_pair[0]
    own_hidden = hidden_pair[0]
    stacked = jnp.concatenate([own_fields, velocity[None, :]], axis=0)
    advanced = advance(extended(stacked, "tile", 1, 1), growth)
    fresh_fields = to_trainer(advanced)
    grad_out, grad_hidden, other_out, other_hidden = plain_training(
        features,
        own_hidden.astype(jnp.bfloat16),
        own_out.astype(jnp.bfloat16),
        own_fields,
        own_out,
        own_hidden,
    )
    grad_out, grad_hidden, other_out, other_hidden = (
        v.astype(jnp.float32) for v in (grad_out, grad_hidden, other_out, other_hidden)
    )
    out_next = jnp.where(
        solver_side,
        momentum_decay * own_out + other_out,
        own_out - step_size * (momentum_decay * other_out + grad_out),
    )
    hidden_next = jnp.where(
        solver_side,
        momentum_decay * own_hidden + other_hidden,
        own_hidden - step_size * (momentum_decay * other_hidden + grad_hidden),
    )
    next_batch = jnp.take(fresh_fields, assignment, axis=0).astype(jnp.float32)
    fields_next = jnp.where(solver_side, advanced, next_batch)
    return (fields_next[None], out_next[None], hidden_next[None])


def solution(mesh):
    return jax.shard_map(
        body,
        mesh=mesh,
        in_specs=(
            P("role", None, "tile"),
            P("tile"),
            P("tile"),
            P(),
            P(),
            P("role", None, "tile"),
            P("role", None, "tile", None),
        ),
        out_specs=(P("role", None, "tile"), P("role", None, "tile"), P("role", None, "tile", None)),
        check_vma=False,
    )
```

time: 473 us -> 391 us (0.83)
  waiting for transfers between devices: 343 us -> 272 us
  matrix products: 0 us -> 52.6 us
  local copies, waits for them, and re-layouts: 41.8 us -> 6.81 us
  starting transfers between devices: 42.1 us -> 22.9 us
  other arithmetic: 30.1 us -> 22 us
    psum x2 -> x1, waiting for transfers between devices: 221 us -> 86 us  [plain_training(): upstream = lax.psum(partial_grad, 'tile')]
    all_gather x1 -> x5, waiting for transfers between devices: 91.3 us -> 166 us  [plain_training(): lax.all_gather(hidden_narrow[i], 'tile', axis=0, tiled=True)]
    dot_general x0 -> x16, matrix products: none -> 52.6 us  [the longest x5 21.8 us: plain_training(): jnp.dot(activation, full_hidden[i], preferred_element_type=jnp.float32)]
    ppermute x1 -> x9, starting transfers between devices: 37.5 us -> 18.1 us  [the longest x3 10.2 us: to_trainer(): return lax.ppermute(value.astype(jnp.bfloat16), 'role', [(0, 1)])]
    ppermute x1 -> x9, waiting for transfers between devices: 28.6 us -> 11.5 us  [the longest x6 11.5 us: to_solver(): return lax.ppermute(value.astype(jnp.bfloat16), 'role', [(1, 0)])]
    another operation x5 -> x1, local copies, waits for them, and re-layouts: 13.6 us -> 0.01 us  [plain_training(): jnp.stack(sent[::-1])]
    slice x4 -> x1, local copies, waits for them, and re-layouts: 11.1 us -> 0.84 us  [plain_training(): hidden_narrow[i]]
    select_n x3 -> x1, other arithmetic: 9.54 us -> 0.01 us  [body(): next_batch = jnp.take(fresh_fields, assignment, axis=0).astype(jnp.float32)]
  transfers between devices with their start and end apart: 6 -> 17, of which waited for: 5 -> 11; matrix products, arithmetic and copies ran while one was open for 5% -> 18% of each run, Pallas kernels for 0% -> 0%
where the time goes in v1:
time: 391 us
  waiting for transfers between devices  272 us (70%)
  matrix products  52.6 us (13%)
  starting transfers between devices  22.9 us (6%)
  other arithmetic  22 us (6%)
  between operations  14.6 us (4%)
  local copies, waits for them, and re-layouts  6.81 us (2%)
    all_gather x5, waiting for transfers between devices, plain_training(): lax.all_gather(hidden_narrow[i], 'tile', axis=0, tiled=True)  166 us
    psum x1, waiting for transfers between devices, plain_training(): upstream = lax.psum(partial_grad, 'tile')  86 us
    dot_general x5, matrix products, plain_training(): jnp.dot(activation, full_hidden[i], preferred_element_type=jnp.float32)  21.8 us
    ppermute x6, waiting for transfers between devices, to_solver(): return lax.ppermute(value.astype(jnp.bfloat16), 'role', [(1, 0)])  11.5 us
    dot_general x5, matrix products, plain_training(): gradient = jnp.dot(own_inputs.T, slope, preferred_element_type=jnp.float32)  10.8 us
    broadcast_in_dim x3, other arithmetic, body(): return (fields_next[None], out_next[None], hidden_next[None])  10.3 us
    ppermute x3, starting transfers between devices, to_trainer(): return lax.ppermute(value.astype(jnp.bfloat16), 'role', [(0, 1)])  10.2 us
    dot_general x3, matrix products, plain_training(): lax.dot_general(slope, full_hidden[i], (((1,), (1,)), ((), ())), preferre...  8.2 us
  transfers between devices with their start and end apart: 17, of which 11 were waited for; matrix products, arithmetic and copies ran while one was open for 18% of the time, Pallas kernels for 0%

profile of v1, /device:TPU:0, one launch (start us, length us, event | category | flops | bytes accessed | tf_op | source)
XLA Modules:
  0.0 390.6 jit_solution(13564146009136946338)
XLA Ops:
  13.1 5.9 %collective-permute-start.10 = (bf16[5,64,1024]{2,1,0:T(8,128)(2,1)}, bf16[5,64,1024]{2,1,0:T(8,128)(2,1)}, u32[]{:S(2)}, u32[]{:S(2)}) collective-permute-start(bf16[5,64,1024]{2,1,0:T(8,128)(2,1)} %copy-done.6), channel_id=1, source_target_pairs={{0,16},{1,17},{2,18},{3,19},{4,20},{5,21},{6,22},{7,23},{8,24},{9,... | collective-permute-start | bytes 1966088 | tf_op jit(solution)/shard_map/ppermute | solution.py:38
  19.0 4.0 %bitcast_convert_fusion = bf16[1024,1024]{1,0:T(8,128)(2,1)} fusion(f32[1,1024,1024]{2,1,0:T(8,128)} %param.12), kind=kLoop, calls=%fused_computation.8 | loop fusion | flops 1048576 | bytes 6291456 | tf_op jit(solution)/shard_map/convert_element_type | solution.py:97
  23.0 2.8 collective-permute-start.4
  26.0 4.4 %collective-permute-start.1 = (f32[513,1]{1,0:T(8,128)S(1)}, f32[513,1]{1,0:T(8,128)S(1)}, u32[]{:S(2)}, u32[]{:S(2)}) collective-permute-start(f32[513,1]{1,0:T(8,128)S(1)} %get-tuple-element.8), channel_id=1, source_target_pairs={{1,0},{2,1},{3,2},{4,3},{5,4},{6,5},{7,6},{8,7},{9,8},{10,9},{11,1... | collective-permute-start | bytes 6164 | tf_op jit(solution)/shard_map/ppermute | solution.py:17
  30.4 5.4 %collective-permute-done = f32[513,1]{1,0:T(8,128)S(1)} collective-permute-done((f32[513,1]{1,0:T(8,128)S(1)}, f32[513,1]{1,0:T(8,128)S(1)}, u32[]{:S(2)}, u32[]{:S(2)}) %collective-permute-start) | collective-permute-done | bytes 2084 | tf_op jit(solution)/shard_map/ppermute | solution.py:16
  36.7 2.4 fusion.59
  40.6 15.2 %all-gather.11.cloned.1.call-done = bf16[1,1024,1024]{2,1,0:T(8,128)(2,1)} async-done(((bf16[1,64,1024]{2,1,0:T(8,128)(2,1)}), bf16[1,1024,1024]{2,1,0:T(8,128)(2,1)}) %all-gather.11.cloned.1.call-update) | async-done | bytes 2097168 | tf_op jit(solution)/shard_map/all_gather | solution.py:52
  55.8 4.6 %multiply_convert_fusion.10 = (bf16[512,1024]{1,0:T(8,128)(2,1)}, f32[512,1024]{1,0:T(8,128)}) fusion(bf16[512,1024]{1,0:T(8,128)(2,1)S(1)} %copy-done, bf16[1,1024,1024]{2,1,0:T(8,128)(2,1)} %all-gather.11.cloned.1.call-done), kind=kOutput, calls=%fused_computation.51 | convolution fusion | flops 1076363264 | bytes 6291456 | tf_op jit(solution)/shard_map/dot_general | solution.py:58
  60.5 37.8 %all-gather.13.cloned.1.call-done = bf16[1,1024,1024]{2,1,0:T(8,128)(2,1)} async-done(((bf16[1,64,1024]{2,1,0:T(8,128)(2,1)}), bf16[1,1024,1024]{2,1,0:T(8,128)(2,1)}) %all-gather.13.cloned.1.call-update) | async-done | bytes 2097168 | tf_op jit(solution)/shard_map/all_gather | solution.py:52
  98.2 4.7 %multiply_convert_fusion.9 = (bf16[512,1024]{1,0:T(8,128)(2,1)S(1)}, f32[512,1024]{1,0:T(8,128)}) fusion(bf16[512,1024]{1,0:T(8,128)(2,1)} %get-tuple-element.14, bf16[1,1024,1024]{2,1,0:T(8,128)(2,1)} %all-gather.13.cloned.1.call-done), kind=kOutput, calls=%fused_computation.49 | convolution fusion | flops 1076363264 | bytes 6291456 | tf_op jit(solution)/shard_map/dot_general | solution.py:58
  102.9 37.7 %all-gather.15.cloned.1.call-done = bf16[1,1024,1024]{2,1,0:T(8,128)(2,1)} async-done(((bf16[1,64,1024]{2,1,0:T(8,128)(2,1)}), bf16[1,1024,1024]{2,1,0:T(8,128)(2,1)}) %all-gather.15.cloned.1.call-update) | async-done | bytes 2097168 | tf_op jit(solution)/shard_map/all_gather | solution.py:52
  140.6 4.7 %multiply_convert_fusion.8 = (bf16[512,1024]{1,0:T(8,128)(2,1)}, f32[512,1024]{1,0:T(8,128)}) fusion(bf16[512,1024]{1,0:T(8,128)(2,1)S(1)} %get-tuple-element.16, bf16[1,1024,1024]{2,1,0:T(8,128)(2,1)} %all-gather.15.cloned.1.call-done), kind=kOutput, calls=%fused_computation.47 | convolution fusion | flops 1076363264 | bytes 6291456 | tf_op jit(solution)/shard_map/dot_general | solution.py:58
  145.3 37.5 %all-gather.17.cloned.1.call-done = bf16[1,1024,1024]{2,1,0:T(8,128)(2,1)} async-done(((bf16[1,64,1024]{2,1,0:T(8,128)(2,1)}), bf16[1,1024,1024]{2,1,0:T(8,128)(2,1)}) %all-gather.17.cloned.1.call-update) | async-done | bytes 2097168 | tf_op jit(solution)/shard_map/all_gather | solution.py:52
  182.8 4.7 %multiply_convert_fusion.7 = (bf16[512,1024]{1,0:T(8,128)(2,1)S(1)}, f32[512,1024]{1,0:T(8,128)}) fusion(bf16[512,1024]{1,0:T(8,128)(2,1)} %get-tuple-element.18, bf16[1,1024,1024]{2,1,0:T(8,128)(2,1)} %all-gather.17.cloned.1.call-done), kind=kOutput, calls=%fused_computation.45 | convolution fusion | flops 1076363264 | bytes 6291456 | tf_op jit(solution)/shard_map/dot_general | solution.py:58
  187.6 38.1 %all-gather.19.cloned.1.call-done = bf16[1,1024,1024]{2,1,0:T(8,128)(2,1)} async-done(((bf16[1,64,1024]{2,1,0:T(8,128)(2,1)}), bf16[1,1024,1024]{2,1,0:T(8,128)(2,1)}) %all-gather.19.cloned.1.call-update) | async-done | bytes 2097168 | tf_op jit(solution)/shard_map/all_gather | solution.py:52
  225.6 3.0 fusion.10
  228.7 3.7 multiply_convert_fusion.5
  233.3 4.2 %fusion.64 = f32[512,1024]{1,0:T(8,128)} fusion(bf16[512,1024]{1,0:T(8,128)(2,1)S(1)} %multiply_convert_fusion.5, bf16[1024,1024]{1,0:T(8,128)(2,1)} %bitcast_convert_fusion), kind=kOutput, calls=%fused_computation.103 | convolution fusion | flops 1073741824 | bytes 5242880 | tf_op jit(solution)/shard_map/dot_general | solution.py:63
  237.6 2.1 gather_fusion
  239.6 3.4 select_bitcast_fusion
  243.0 4.1 %fusion.61 = (bf16[1024,1024]{1,0:T(8,128)(2,1)}, f32[1024,1024]{1,0:T(8,128)}) fusion(bf16[512,1024]{1,0:T(8,128)(2,1)S(1)} %copy-done.20, f32[512,1024]{1,0:T(8,128)S(1)} %copy-done.8), kind=kOutput, calls=%fused_computation.102 | convolution fusion | flops 1077411840 | bytes 9437184 | tf_op jit(solution)/shard_map/dot_general | solution.py:67
  248.6 86.0 %all-reduce.2.cloned.1.call-done = f32[512,1024]{1,0:T(8,128)} async-done(((f32[512,1024]{1,0:T(8,128)}), f32[512,1024]{1,0:T(8,128)}) %all-reduce.2.cloned.1.call-update) | async-done | bytes 2097168 | tf_op jit(solution)/shard_map/psum | solution.py:66
  334.6 3.0 multiply_convert_fusion.4
  337.5 4.0 %multiply_convert_fusion.3 = bf16[512,1024]{1,0:T(8,128)(2,1)S(1)} fusion(f32[512,1024]{1,0:T(8,128)} %get-tuple-element.21, bf16[512,1024]{1,0:T(8,128)(2,1)S(1)} %multiply_convert_fusion.4, bf16[1,1024,1024]{2,1,0:T(8,128)(2,1)} %all-gather.19.cloned.1.call-done), kind=kOutput, calls=%fused_computation.40 | convolution fusion | flops 1078460416 | bytes 6291456 | tf_op jit(solution)/shard_map/dot_general | solution.py:77
  344.1 2.6 multiply_convert_fusion.1
  346.7 4.3 %bitcast_dynamic-update-slice_fusion.4 = (f32[5,64,1024]{2,1,0:T(8,128)S(1)}, bf16[64,1024]{1,0:T(8,128)(2,1)S(1)}) fusion(f32[512,1024]{1,0:T(8,128)} %get-tuple-element.15, bf16[512,1024]{1,0:T(8,128)(2,1)} %multiply_convert_fusion.1, bf16[1,1024,1024]{2,1,0:T(8,128)(2,1)} %all-gather.13.cloned.1.call-done, bf16[512,1024]{1,0:T(8,128)(2,1)S(1)} %copy-done, ...), kind=kOutput, calls=%fused_computation.72 | convolution fusion | flops 1145634816 | bytes 5767172 | tf_op jit(solution)/shard_map/dot_general | solution.py:73
  351.1 1.8 bitcast_dynamic-update-slice_fusion.3
  355.5 1.7 bitcast_dynamic-update-slice_fusion.2
  360.2 1.8 collective-permute-done.5
  364.6 4.2 %collective-permute-done.7 = bf16[64,1024]{1,0:T(8,128)(2,1)S(1)} collective-permute-done((bf16[64,1024]{1,0:T(8,128)(2,1)S(1)}, bf16[64,1024]{1,0:T(8,128)(2,1)S(1)}, u32[]{:S(2)}, u32[]{:S(2)}) %collective-permute-start.7) | collective-permute-done | bytes 131104 | tf_op jit(solution)/shard_map/ppermute | solution.py:42
  370.2 5.4 %collective-permute-done.9 = bf16[64,1024]{1,0:T(8,128)(2,1)S(1)} collective-permute-done((bf16[64,1024]{1,0:T(8,128)(2,1)S(1)}, bf16[64,1024]{1,0:T(8,128)(2,1)S(1)}, u32[]{:S(2)}, u32[]{:S(2)}) %collective-permute-start.9) | collective-permute-done | bytes 131104 | tf_op jit(solution)/shard_map/ppermute | solution.py:42
  378.4 5.3 %fusion.1 = f32[1,1024,1024]{2,1,0:T(8,128)} fusion(f32[1024,1024]{1,0:T(8,128)S(1)} %copy-done.5, f32[1,1024,1024]{2,1,0:T(8,128)S(1)} %copy-done.3, bf16[1024,1024]{1,0:T(8,128)(2,1)} %collective-permute-done.3, bf16[1024,1024]{1,0:T(8,128)(2,1)} %collective-permute-done.4, pred[]{:T(512)S(6)} %eq.4), kind=kLoop, calls=%fused_computation.4 | loop fusion | flops 9437184 | bytes 16777216 | tf_op jit(solution)/shard_map/broadcast_in_dim | solution.py:117
  (90 shorter events, 25.7 us)
Async XLA Ops:
  7.2 48.7 %copy-start = (bf16[512,1024]{1,0:T(8,128)(2,1)S(1)}, bf16[512,1024]{1,0:T(8,128)(2,1)}, u32[]{:S(2)}) copy-start(bf16[512,1024]{1,0:T(8,128)(2,1)} %param.10) | copy-start | bytes 3145732
  7.2 48.7 %all-gather.11.cloned.1.call-start = ((), (), s32[]{:S(2)}) async-start(), calls=%async_computation.1 | async-start | bytes 2228224 | tf_op jit(solution)/shard_map/all_gather | solution.py:52
  10.4 87.8 %all-gather.13.cloned.1.call-start = ((), (), s32[]{:S(2)}) async-start(), calls=%async_computation.2 | async-start | bytes 2228224 | tf_op jit(solution)/shard_map/all_gather | solution.py:52
  11.2 129.5 %all-gather.15.cloned.1.call-start = ((), (), s32[]{:S(2)}) async-start(), calls=%async_computation.3 | async-start | bytes 2228224 | tf_op jit(solution)/shard_map/all_gather | solution.py:52
  11.9 170.9 %all-gather.17.cloned.1.call-start = ((), (), s32[]{:S(2)}) async-start(), calls=%async_computation.4 | async-start | bytes 2228224 | tf_op jit(solution)/shard_map/all_gather | solution.py:52
  12.5 213.2 %all-gather.19.cloned.1.call-start = ((), (), s32[]{:S(2)}) async-start(), calls=%async_computation.5 | async-start | bytes 2228224 | tf_op jit(solution)/shard_map/all_gather | solution.py:52
  13.1 12.7 %copy-start.1 = (f32[1,512,1024]{2,1,0:T(8,128)S(1)}, f32[1,512,1024]{2,1,0:T(8,128)}, u32[]{:S(2)}) copy-start(f32[1,512,1024]{2,1,0:T(8,128)} %param.7) | copy-start | bytes 6291460
  13.1 12.7 %copy-start.12 = (f32[1024]{0:T(1024)S(1)}, f32[1024]{0:T(1024)}, u32[]{:S(2)}) copy-start(f32[1024]{0:T(1024)} %param.8) | copy-start | bytes 12292
  13.1 321.5 %all-reduce.2.cloned.1.call-start = ((), (), s32[]{:S(2)}) async-start(), calls=%async_computation | async-start | bytes 4194304 | tf_op jit(solution)/shard_map/psum | solution.py:66
  13.1 362.6 %collective-permute-start.10 = (bf16[5,64,1024]{2,1,0:T(8,128)(2,1)}, bf16[5,64,1024]{2,1,0:T(8,128)(2,1)}, u32[]{:S(2)}, u32[]{:S(2)}) collective-permute-start(bf16[5,64,1024]{2,1,0:T(8,128)(2,1)} %copy-done.6), channel_id=1, source_target_pairs={{0,16},{1,17},{2,18},{3,19},{4,20},{5,21},{6,22},{7,23},{8,24},{9,... | collective-permute-start | bytes 1966088 | tf_op jit(solution)/shard_map/ppermute | solution.py:38
  23.0 7.4 %copy-start.15 = (s32[512]{0:T(512)S(1)}, s32[512]{0:T(512)}, u32[]{:S(2)}) copy-start(s32[512]{0:T(512)} %param.11) | copy-start | bytes 6148
  23.0 354.3 %collective-permute-start.4 = (bf16[1024,1024]{1,0:T(8,128)(2,1)}, bf16[1024,1024]{1,0:T(8,128)(2,1)}, u32[]{:S(2)}, u32[]{:S(2)}) collective-permute-start(bf16[1024,1024]{1,0:T(8,128)(2,1)} %bitcast_convert_fusion), channel_id=1, source_target_pairs={{0,16},{1,17},{2,18},{3,19},{4,20},{5,21},{6,22},{7,23},{8,24},{9,... | collective-permute-start | bytes 6291464 | tf_op jit(solution)/shard_map/ppermute | solution.py:38
  25.9 9.9 %collective-permute-start = (f32[513,1]{1,0:T(8,128)S(1)}, f32[513,1]{1,0:T(8,128)S(1)}, u32[]{:S(2)}, u32[]{:S(2)}) collective-permute-start(f32[513,1]{1,0:T(8,128)S(1)} %get-tuple-element.7), channel_id=1, source_target_pairs={{0,1},{1,2},{2,3},{3,4},{4,5},{5,6},{6,7},{7,8},{8,9},{9,10},{10,1... | collective-permute-start | bytes 6164 | tf_op jit(solution)/shard_map/ppermute | solution.py:16
  26.0 10.0 %collective-permute-start.1 = (f32[513,1]{1,0:T(8,128)S(1)}, f32[513,1]{1,0:T(8,128)S(1)}, u32[]{:S(2)}, u32[]{:S(2)}) collective-permute-start(f32[513,1]{1,0:T(8,128)S(1)} %get-tuple-element.8), channel_id=1, source_target_pairs={{1,0},{2,1},{3,2},{4,3},{5,4},{6,5},{7,6},{8,7},{9,8},{10,9},{11,1... | collective-permute-start | bytes 6164 | tf_op jit(solution)/shard_map/ppermute | solution.py:17
  39.1 198.5 %collective-permute-start.2 = (bf16[512,1024]{1,0:T(8,128)(2,1)}, bf16[512,1024]{1,0:T(8,128)(2,1)S(1)}, u32[]{:S(2)}, u32[]{:S(2)}) collective-permute-start(bf16[512,1024]{1,0:T(8,128)(2,1)} %get-tuple-element.5), channel_id=1, source_target_pairs={{0,16},{1,17},{2,18},{3,19},{4,20},{5,21},{6,22},{7,23},{8,24},{9,... | collective-permute-start | bytes 3145736 | tf_op jit(solution)/shard_map/ppermute | solution.py:38
  102.9 42.4 %copy-start.13 = (bf16[512,1024]{1,0:T(8,128)(2,1)}, bf16[512,1024]{1,0:T(8,128)(2,1)S(1)}, u32[]{:S(2)}) copy-start(bf16[512,1024]{1,0:T(8,128)(2,1)S(1)} %get-tuple-element.16) | copy-start | bytes 3145732
  187.5 41.1 %copy-start.14 = (bf16[512,1024]{1,0:T(8,128)(2,1)}, bf16[512,1024]{1,0:T(8,128)(2,1)S(1)}, u32[]{:S(2)}) copy-start(bf16[512,1024]{1,0:T(8,128)(2,1)S(1)} %get-tuple-element.20) | copy-start | bytes 3145732
  228.6 3.7 copy-start.7
  239.6 3.4 copy-start.8
  239.6 3.4 copy-start.20
  247.1 130.3 %collective-permute-start.3 = (bf16[1024,1024]{1,0:T(8,128)(2,1)}, bf16[1024,1024]{1,0:T(8,128)(2,1)}, u32[]{:S(2)}, u32[]{:S(2)}) collective-permute-start(bf16[1024,1024]{1,0:T(8,128)(2,1)} %get-tuple-element.22), channel_id=1, source_target_pairs={{16,0},{17,1},{18,2},{19,3},{20,4},{21,5},{22,6},{23,7},{24,8},{25... | collective-permute-start | bytes 6291464 | tf_op jit(solution)/shard_map/ppermute | solution.py:42
  337.5 4.0 %copy-start.18 = (bf16[1,1024,1024]{2,1,0:T(8,128)(2,1)S(1)}, bf16[1,1024,1024]{2,1,0:T(8,128)(2,1)}, u32[]{:S(2)}) copy-start(bf16[1,1024,1024]{2,1,0:T(8,128)(2,1)} %all-gather.17.cloned.1.call-done) | copy-start | bytes 6291460
  337.5 4.0 %copy-start.22 = (f32[512,1024]{1,0:T(8,128)S(1)}, f32[512,1024]{1,0:T(8,128)}, u32[]{:S(2)}) copy-start(f32[512,1024]{1,0:T(8,128)} %get-tuple-element.19) | copy-start | bytes 6291460
  343.2 3.5 copy-start.11
  351.1 6.1 %copy-start.10 = (bf16[512,1024]{1,0:T(8,128)(2,1)S(1)}, bf16[512,1024]{1,0:T(8,128)(2,1)}, u32[]{:S(2)}) copy-start(bf16[512,1024]{1,0:T(8,128)(2,1)} %copy-done.9) | copy-start | bytes 3145732
  352.9 10.4 %collective-permute-start.6 = (bf16[64,1024]{1,0:T(8,128)(2,1)S(1)}, bf16[64,1024]{1,0:T(8,128)(2,1)S(1)}, u32[]{:S(2)}, u32[]{:S(2)}) collective-permute-start(bf16[64,1024]{1,0:T(8,128)(2,1)S(1)} %get-tuple-element.27), channel_id=1, source_target_pairs={{16,0},{17,1},{18,2},{19,3},{20,4},{21,5},{22,6},{23,7},{24,8},{25... | collective-permute-start | bytes 393224 | tf_op jit(solution)/shard_map/ppermute | solution.py:42
  354.2 7.8 %collective-permute-start.5 = (bf16[64,1024]{1,0:T(8,128)(2,1)S(1)}, bf16[64,1024]{1,0:T(8,128)(2,1)S(1)}, u32[]{:S(2)}, u32[]{:S(2)}) collective-permute-start(bf16[64,1024]{1,0:T(8,128)(2,1)S(1)} %get-tuple-element.25), channel_id=1, source_target_pairs={{16,0},{17,1},{18,2},{19,3},{20,4},{21,5},{22,6},{23,7},{24,8},{25... | collective-permute-start | bytes 393224 | tf_op jit(solution)/shard_map/ppermute | solution.py:42
  357.2 18.5 %copy-start.4 = (f32[1,5,64,1024]{3,2,1,0:T(8,128)S(1)}, f32[1,5,64,1024]{3,2,1,0:T(8,128)}, u32[]{:S(2)}) copy-start(f32[1,5,64,1024]{3,2,1,0:T(8,128)} %param.13) | copy-start | bytes 3932164
  357.2 20.1 %copy-start.5 = (f32[1024,1024]{1,0:T(8,128)S(1)}, f32[1024,1024]{1,0:T(8,128)}, u32[]{:S(2)}) copy-start(f32[1024,1024]{1,0:T(8,128)} %get-tuple-element.23) | copy-start | bytes 12582916
  362.0 6.8 %collective-permute-start.7 = (bf16[64,1024]{1,0:T(8,128)(2,1)S(1)}, bf16[64,1024]{1,0:T(8,128)(2,1)S(1)}, u32[]{:S(2)}, u32[]{:S(2)}) collective-permute-start(bf16[64,1024]{1,0:T(8,128)(2,1)S(1)} %get-tuple-element.29), channel_id=1, source_target_pairs={{16,0},{17,1},{18,2},{19,3},{20,4},{21,5},{22,6},{23,7},{24,8},{25... | collective-permute-start | bytes 393224 | tf_op jit(solution)/shard_map/ppermute | solution.py:42
  363.3 6.9 %collective-permute-start.8 = (bf16[64,1024]{1,0:T(8,128)(2,1)S(1)}, bf16[64,1024]{1,0:T(8,128)(2,1)S(1)}, u32[]{:S(2)}, u32[]{:S(2)}) collective-permute-start(bf16[64,1024]{1,0:T(8,128)(2,1)S(1)} %get-tuple-element.31), channel_id=1, source_target_pairs={{16,0},{17,1},{18,2},{19,3},{20,4},{21,5},{22,6},{23,7},{24,8},{25... | collective-permute-start | bytes 393224 | tf_op jit(solution)/shard_map/ppermute | solution.py:42
  368.8 6.8 %collective-permute-start.9 = (bf16[64,1024]{1,0:T(8,128)(2,1)S(1)}, bf16[64,1024]{1,0:T(8,128)(2,1)S(1)}, u32[]{:S(2)}, u32[]{:S(2)}) collective-permute-start(bf16[64,1024]{1,0:T(8,128)(2,1)S(1)} %get-tuple-element.33), channel_id=1, source_target_pairs={{16,0},{17,1},{18,2},{19,3},{20,4},{21,5},{22,6},{23,7},{24,8},{25... | collective-permute-start | bytes 393224 | tf_op jit(solution)/shard_map/ppermute | solution.py:42
  (8 other events, 14.4 us)
Sparse Core Ops, SparseCore 0:
  10.5 45.2 all-gather.10
  58.0 40.1 all-gather.12
  100.4 40.1 all-gather.14
  142.6 40.1 all-gather.16
  185.4 40.1 all-gather.18
  237.6 96.8 all-reduce.1

commit v2 on v1

--- a/solution.py
+++ b/solution.py
@@ -1,6 +1,10 @@
+import functools
+
 import jax
 import jax.numpy as jnp
 from jax import lax
+from jax.experimental import pallas as pl
+from jax.experimental.pallas import tpu as pltpu
 from jax.sharding import PartitionSpec as P
 
 momentum_decay = 0.9
@@ -83,6 +87,336 @@
     return grad_out, jnp.stack(gradients[::-1]), other_out, other_hidden
 
 
+LANES = 128
+COLUMNS = 256
+
+
+def train_kernel(
+    groups,
+    features_ref,
+    hidden_ref,
+    out_ref,
+    target_ref,
+    sent_out_ref,
+    sent_hidden_ref,
+    got_out_ref,
+    got_hidden_ref,
+    weights,
+    inputs,
+    factors,
+    residual,
+    partial,
+    slope,
+    payload,
+    payload_hidden,
+    gradient,
+    core_sum,
+    x_sum,
+    z_sum,
+    gather_send,
+    gather_recv,
+    sum_send,
+    sum_recv,
+    slope_send,
+    slope_recv,
+    role_send,
+    role_recv,
+    local_sem,
+):
+    layer_count, unit_rows, width = hidden_ref.shape
+    batch = features_ref.shape[0]
+    rows = partial.shape[3]
+    role = lax.axis_index("role")
+    tile = lax.axis_index("tile")
+    core = lax.rem(tile, 2)
+    x = lax.rem(tile // 2, 2)
+    z = tile // 4
+    solver_side = role == 0
+
+    def device(z_at, x_at, core_at):
+        return (role, z_at * 4 + x_at * 2 + core_at)
+
+    z_places = [lax.rem(z + k, groups) for k in range(1, groups)]
+    z_peers = [device(place, x, core) for place in z_places]
+    x_peer = device(z, 1 - x, core)
+    core_peer = device(z, x, 1 - core)
+    role_peer = (1 - role, tile)
+
+    def send(source, target, send_sem, recv_sem, peer):
+        copy = pltpu.make_async_remote_copy(
+            src_ref=source,
+            dst_ref=target,
+            send_sem=send_sem,
+            recv_sem=recv_sem,
+            device_id=peer,
+            device_id_type=pl.DeviceIdType.MESH,
+        )
+        copy.start()
+        return copy
+
+    own = pltpu.make_async_copy(hidden_ref, weights.at[:, z, x, core], local_sem.at[0])
+    own.start()
+    barrier = pltpu.get_barrier_semaphore()
+    peers = z_peers + [x_peer, core_peer, role_peer]
+    for peer in peers:
+        pl.semaphore_signal(barrier, inc=1, device_id=peer, device_id_type=pl.DeviceIdType.MESH)
+    pl.semaphore_wait(barrier, len(peers))
+
+    sends = []
+    z_copies = []
+    for i in range(layer_count):
+        z_copies.append(
+            [
+                send(
+                    hidden_ref.at[i],
+                    weights.at[i, z, x, core],
+                    gather_send.at[i, k],
+                    gather_recv.at[i, k],
+                    z_peers[k],
+                )
+                for k in range(groups - 1)
+            ]
+        )
+        sends += z_copies[-1]
+    own.wait()
+
+    def columns_of(j):
+        return pl.ds(pl.multiple_of(j * COLUMNS, COLUMNS), COLUMNS)
+
+    def forward(i):
+        @pl.loop(0, width // COLUMNS)
+        def _(j):
+            columns = columns_of(j)
+            block = weights[i, :, :, :, :, columns].reshape(width, COLUMNS)
+            activation = features_ref[...] if i == 0 else inputs[i - 1]
+            summed = jnp.dot(activation, block, preferred_element_type=jnp.float32)
+            logistic = jax.nn.sigmoid(summed)
+            inputs[i, :, columns] = (summed * logistic).astype(jnp.bfloat16)
+            factors[i, :, columns] = logistic * (1.0 + summed * (1.0 - logistic))
+
+    x_copies, core_copies = [], []
+    for i in range(layer_count + 2):
+        if i < layer_count:
+            for copy in z_copies[i]:
+                copy.wait_recv()
+            view = weights.at[i, :, x, core]
+            x_copies.append(
+                send(view, view, gather_send.at[i, groups - 1], gather_recv.at[i, groups - 1], x_peer)
+            )
+        if 1 <= i <= layer_count:
+            x_copies[i - 1].wait_recv()
+            view = weights.at[i - 1, :, :, core]
+            core_copies.append(
+                send(
+                    view,
+                    view,
+                    gather_send.at[i - 1, groups],
+                    gather_recv.at[i - 1, groups],
+                    core_peer,
+                )
+            )
+        if i >= 2:
+            core_copies[i - 2].wait_recv()
+            forward(i - 2)
+    sends += x_copies + core_copies
+
+    last = layer_count - 1
+
+    @pl.loop(0, width // COLUMNS)
+    def _(j):
+        columns = columns_of(j)
+        predicted = jnp.dot(inputs[last], out_ref[:, columns], preferred_element_type=jnp.float32)
+        residual[:, columns] = ((predicted - target_ref[:, columns]) / batch).astype(jnp.bfloat16)
+
+    @pl.loop(0, width // COLUMNS)
+    def _(j):
+        columns = columns_of(j)
+        part = lax.dot_general(
+            residual[...],
+            out_ref[columns, :],
+            (((1,), (1,)), ((), ())),
+            preferred_element_type=jnp.float32,
+        )
+        partial[:, :, :, :, columns] = part.reshape(groups, 2, 2, rows, COLUMNS)
+
+    core_copy = send(
+        partial.at[:, :, 1 - core], core_sum, sum_send.at[0], sum_recv.at[0], core_peer
+    )
+
+    @pl.loop(0, width // COLUMNS)
+    def _(j):
+        columns = columns_of(j)
+        grad = lax.dot_general(
+            inputs[last],
+            residual[:, columns],
+            (((0,), (0,)), ((), ())),
+            preferred_element_type=jnp.float32,
+        )
+        payload[:, columns] = jnp.where(solver_side, out_ref[:, columns], grad.astype(jnp.bfloat16))
+
+    core_copy.wait_recv()
+    away = partial[:, 1 - x, core] + core_sum[:, 1 - x]
+    partial[:, 1 - x, core] = away
+    x_copy = send(partial.at[:, 1 - x, core], x_sum, sum_send.at[1], sum_recv.at[1], x_peer)
+    out_copy = send(payload, got_out_ref, role_send.at[0], role_recv.at[0], role_peer)
+    out_keep = pltpu.make_async_copy(payload, sent_out_ref, local_sem.at[0])
+    out_keep.start()
+    partial[:, x, core] = partial[:, x, core] + core_sum[:, x]
+    x_copy.wait_recv()
+    partial[:, x, core] = partial[:, x, core] + x_sum[...]
+    z_sums = [
+        send(
+            partial.at[z_places[k], x, core],
+            z_sum.at[k],
+            sum_send.at[2 + k],
+            sum_recv.at[2 + k],
+            z_peers[k],
+        )
+        for k in range(groups - 1)
+    ]
+    upstream = partial[z, x, core]
+    for k in range(groups - 1):
+        z_sums[k].wait_recv()
+        upstream = upstream + z_sum[k]
+    own_rows = pl.ds(pl.multiple_of(tile * rows, rows), rows)
+    slope[z, x, core] = (upstream * factors[last, own_rows, :]).astype(jnp.bfloat16)
+    view = slope.at[z, x, core]
+    z_slopes = [
+        send(view, view, slope_send.at[k], slope_recv.at[k], z_peers[k]) for k in range(groups - 1)
+    ]
+    for copy in z_slopes:
+        copy.wait_recv()
+    view = slope.at[:, x, core]
+    x_slope = send(view, view, slope_send.at[groups - 1], slope_recv.at[groups - 1], x_peer)
+    x_slope.wait_recv()
+    view = slope.at[:, :, core]
+    core_slope = send(view, view, slope_send.at[groups], slope_recv.at[groups], core_peer)
+    core_slope.wait_recv()
+    sends += [core_copy, x_copy, out_copy] + z_sums
+    for copy in z_slopes + [x_slope, core_slope]:
+        copy.wait_send()
+
+    per_block = LANES // unit_rows
+    first_lane = pl.multiple_of((tile // per_block) * LANES, LANES)
+    unit_first = pl.multiple_of(lax.rem(tile, per_block) * unit_rows, unit_rows)
+    role_copies = []
+    for i in reversed(range(layer_count)):
+        source = features_ref if i == 0 else inputs.at[i - 1]
+        own_inputs = source[:, pl.ds(first_lane, LANES)]
+
+        @pl.loop(0, width // COLUMNS)
+        def _(j):
+            columns = columns_of(j)
+            gradient[:, columns] = lax.dot_general(
+                own_inputs,
+                slope[:, :, :, :, columns].reshape(batch, COLUMNS),
+                (((0,), (0,)), ((), ())),
+                preferred_element_type=jnp.float32,
+            )
+
+        mine = gradient[pl.ds(unit_first, unit_rows), :].astype(jnp.bfloat16)
+        payload_hidden[i] = jnp.where(solver_side, hidden_ref[i], mine)
+        if i > 0:
+            whole_slope = slope[...].reshape(batch, width)
+
+            @pl.loop(0, width // COLUMNS)
+            def _(j):
+                columns = columns_of(j)
+                block = weights.at[i].reshape(width, width)[columns, :]
+                back = lax.dot_general(
+                    whole_slope,
+                    block,
+                    (((1,), (1,)), ((), ())),
+                    preferred_element_type=jnp.float32,
+                )
+                residual[:, columns] = (back * factors[i - 1, :, columns]).astype(jnp.bfloat16)
+
+        role_copies.append(
+            send(
+                payload_hidden.at[i],
+                got_hidden_ref.at[i],
+                role_send.at[1 + i],
+                role_recv.at[1 + i],
+                role_peer,
+            )
+        )
+        if i > 0:
+            slope[...] = residual[...].reshape(slope.shape)
+    hidden_keep = pltpu.make_async_copy(payload_hidden, sent_hidden_ref, local_sem.at[1])
+    hidden_keep.start()
+    sends += role_copies
+    out_copy.wait_recv()
+    for copy in role_copies:
+        copy.wait_recv()
+    for copy in sends:
+        copy.wait_send()
+    out_keep.wait()
+    hidden_keep.wait()
+
+
+def fused_training(features, hidden_narrow, out_narrow, own_fields, own_out, own_hidden):
+    layer_count, unit_rows, width = hidden_narrow.shape
+    batch, cells = own_fields.shape
+    groups = lax.axis_size("tile") // 4
+    rows = batch // lax.axis_size("tile")
+    narrow, wide = jnp.bfloat16, jnp.float32
+    dma = pltpu.SemaphoreType.DMA
+    vmem = pl.BlockSpec(memory_space=pltpu.VMEM)
+    anywhere = pl.BlockSpec(memory_space=pl.ANY)
+    return pl.pallas_call(
+        functools.partial(train_kernel, groups),
+        out_shape=(
+            jax.ShapeDtypeStruct((width, cells), narrow),
+            jax.ShapeDtypeStruct(hidden_narrow.shape, narrow),
+            jax.ShapeDtypeStruct((width, cells), narrow),
+            jax.ShapeDtypeStruct(hidden_narrow.shape, narrow),
+        ),
+        in_specs=[vmem] * 4,
+        out_specs=[anywhere] * 4,
+        scratch_shapes=[
+            pltpu.VMEM((layer_count, groups, 2, 2, unit_rows, width), narrow),
+            pltpu.VMEM((layer_count, batch, width), narrow),
+            pltpu.VMEM((layer_count, batch, width), wide),
+            pltpu.VMEM((batch, cells), narrow),
+            pltpu.VMEM((groups, 2, 2, rows, width), wide),
+            pltpu.VMEM((groups, 2, 2, rows, width), narrow),
+            pltpu.VMEM((width, cells), narrow),
+            pltpu.VMEM(hidden_narrow.shape, narrow),
+            pltpu.VMEM((LANES, width), wide),
+            pltpu.VMEM((groups, 2, rows, width), wide),
+            pltpu.VMEM((groups, rows, width), wide),
+            pltpu.VMEM((groups - 1, rows, width), wide),
+            dma((layer_count, groups + 1)),
+            dma((layer_count, groups + 1)),
+            dma((groups + 1,)),
+            dma((groups + 1,)),
+            dma((groups + 1,)),
+            dma((groups + 1,)),
+            dma((layer_count + 1,)),
+            dma((layer_count + 1,)),
+            dma((2,)),
+        ],
+        compiler_params=pltpu.CompilerParams(
+            collective_id=0, has_side_effects=True, vmem_limit_bytes=64000000
+        ),
+        cost_estimate=pl.CostEstimate(
+            flops=60 * batch * width * width, bytes_accessed=40 * batch * width, transcendentals=0
+        ),
+    )(features, hidden_narrow, out_narrow, own_fields)
+
+
+def training(features, hidden_narrow, out_narrow, own_fields, own_out, own_hidden):
+    tiles = lax.axis_size("tile")
+    fits = (
+        tiles % 4 == 0
+        and tiles > 4
+        and (own_fields.shape[0] // tiles) % 16 == 0
+        and LANES % own_hidden.shape[1] == 0
+    )
+    chosen = fused_training if fits else plain_training
+    return chosen(features, hidden_narrow, out_narrow, own_fields, own_out, own_hidden)
+
+
 def body(fields_pair, velocity, growth, features, assignment, out_pair, hidden_pair):
     solver_side = lax.axis_index("role") == 0
     own_fields = fields_pair[0]
@@ -91,7 +425,7 @@
     stacked = jnp.concatenate([own_fields, velocity[None, :]], axis=0)
     advanced = advance(extended(stacked, "tile", 1, 1), growth)
     fresh_fields = to_trainer(advanced)
-    grad_out, grad_hidden, other_out, other_hidden = plain_training(
+    grad_out, grad_hidden, other_out, other_hidden = training(
         features,
         own_hidden.astype(jnp.bfloat16),
         own_out.astype(jnp.bfloat16),

time: 391 us -> 205 us (0.52)
  waiting for transfers between devices: 272 us -> 13.3 us
  Pallas kernels: 0 us -> 157 us
  matrix products: 52.6 us -> 0 us
  between operations: 14.6 us -> 0.76 us
  starting transfers between devices: 22.9 us -> 9.16 us
  local copies, waits for them, and re-layouts: 6.81 us -> 2.8 us
    all_gather x5 -> x0, waiting for transfers between devices: 166 us -> none  [plain_training(): lax.all_gather(hidden_narrow[i], 'tile', axis=0, tiled=True)]
    pallas_call x0 -> x1, Pallas kernels: none -> 157 us  [fused_training(): pl.pallas_call(functools.partial(train_kernel, groups), out_shape=(jax.Sh...]
    psum x1 -> x0, waiting for transfers between devices: 86 us -> none  [plain_training(): upstream = lax.psum(partial_grad, 'tile')]
    dot_general x16 -> x0, matrix products: 52.6 us -> none  [the longest x5 21.8 us: plain_training(): jnp.dot(activation, full_hidden[i], preferred_element_type=jnp.float32)]
    ppermute x3 -> x1, waiting for transfers between devices: 0.01 us -> 13.3 us  [to_trainer(): return lax.ppermute(value.astype(jnp.bfloat16), 'role', [(0, 1)])]
    ppermute x6 -> x0, waiting for transfers between devices: 11.5 us -> none  [to_solver(): return lax.ppermute(value.astype(jnp.bfloat16), 'role', [(1, 0)])]
    ppermute x6 -> x0, starting transfers between devices: 7.94 us -> none  [to_solver(): return lax.ppermute(value.astype(jnp.bfloat16), 'role', [(1, 0)])]
    ppermute x3 -> x1, starting transfers between devices: 10.2 us -> 3.72 us  [to_trainer(): return lax.ppermute(value.astype(jnp.bfloat16), 'role', [(0, 1)])]
  transfers between devices with their start and end apart: 17 -> 3, of which waited for: 11 -> 1; matrix products, arithmetic and copies ran while one was open for 18% -> 6% of each run, Pallas kernels for 0% -> 77%
where the time goes in v2:
time: 205 us
  Pallas kernels  157 us (77%)
  other arithmetic  21.3 us (10%)
  waiting for transfers between devices  13.3 us (6%)
  starting transfers between devices  9.16 us (4%)
  local copies, waits for them, and re-layouts  2.8 us (1%)
    pallas_call x1, Pallas kernels, fused_training(): pl.pallas_call(functools.partial(train_kernel, groups), out_shape=(jax.Sh...  157 us
    ppermute x1, waiting for transfers between devices, to_trainer(): return lax.ppermute(value.astype(jnp.bfloat16), 'role', [(0, 1)])  13.3 us
    broadcast_in_dim x3, other arithmetic, body(): return (fields_next[None], out_next[None], hidden_next[None])  12.1 us
    ppermute x1, starting transfers between devices, extended(): after = lax.ppermute(leading, axis, down)  4.95 us
  transfers between devices with their start and end apart: 3, of which 1 were waited for; matrix products, arithmetic and copies ran while one was open for 6% of the time, Pallas kernels for 77%

profile of v2, /device:TPU:0, one launch (start us, length us, event | category | flops | bytes accessed | tf_op | source)
XLA Modules:
  0.0 204.7 jit_solution(14084980014657675567)
XLA Ops:
  0.6 0.0 copy-start.1
  0.6 2.1 %pad_maximum_fusion.5 = (f32[513,1]{1,0:T(8,128)}, f32[513,1]{1,0:T(8,128)S(1)}) fusion(f32[1,1024]{1,0:T(1,128)} %bitcast.26, f32[512,1024]{1,0:T(8,128)} %bitcast.22), kind=kLoop, calls=%fused_computation.31 | loop fusion | flops 1026 | bytes 2105352 | tf_op jit(solution)/shard_map/slice | solution.py:18
  2.7 0.5 collective-permute-start
  3.2 5.0 %collective-permute-start.1 = (f32[513,1]{1,0:T(8,128)S(1)}, f32[513,1]{1,0:T(8,128)S(1)}, u32[]{:S(2)}, u32[]{:S(2)}) collective-permute-start(f32[513,1]{1,0:T(8,128)S(1)} %get-tuple-element.16), channel_id=1, source_target_pairs={{1,0},{2,1},{3,2},{4,3},{5,4},{6,5},{7,6},{8,7},{9,8},{10,9},{11,1... | collective-permute-start | bytes 6164 | tf_op jit(solution)/shard_map/ppermute | solution.py:21
  8.2 2.3 %bitcast_convert_fusion.1.hidden_ref = bf16[5,64,1024]{2,1,0:T(8,128)(2,1)} fusion(f32[1,5,64,1024]{3,2,1,0:T(8,128)} %param.13), kind=kLoop, calls=%fused_computation.29 | loop fusion | flops 327680 | bytes 1966080 | tf_op jit(solution)/shard_map/convert_element_type | solution.py:430
  10.4 0.0 copy-done.1
  10.4 1.7 bitcast_convert_fusion.out_ref
  12.1 0.0 copy-start.5
  12.1 0.0 copy-start
  12.1 0.0 copy-start.4
  12.1 157.4 %shard_map.94 = (bf16[1024,1024]{1,0:T(8,128)(2,1)}, bf16[5,64,1024]{2,1,0:T(8,128)(2,1)}, bf16[1024,1024]{1,0:T(8,128)(2,1)}, bf16[5,64,1024]{2,1,0:T(8,128)(2,1)}) custom-call(bf16[512,1024]{1,0:T(8,128)(2,1)} %features_ref.1, bf16[5,64,1024]{2,1,0:T(8,128)(2,1)} %bitcast_convert_fusion.1.hidden_ref, bf16[1024,1024]{1,0:T(8,128)(2,1)} %bitcast_convert_fusion.out_ref, ...), custom_call_target="tpu_custom_call" | custom-call | flops 32212254720 | bytes 20971520 | tf_op jit(solution)/shard_map/pallas_call | solution.py:366
  169.5 0.0 copy-done.5
  169.5 0.0 collective-permute-done
  169.5 0.0 copy-done
  169.6 0.0 copy-done.4
  169.6 0.1 maximum_reduce_fusion
  169.7 0.0 collective-permute-done.1
  169.7 0.0 copy-start.6
  169.7 0.7 fusion.6
  170.4 0.0 copy-done.6
  170.4 2.4 %fusion.13 = (bf16[512,1024]{1,0:T(8,128)(2,1)}, f32[512,1024]{1,0:T(8,128)}) fusion(f32[1024]{0:T(1024)S(1)} %copy-done.6, f32[512,1025]{1,0:T(8,128)S(1)} %fusion.6, f32[1,512,1024]{2,1,0:T(8,128)S(1)} %copy-done), kind=kLoop, calls=%fused_computation.38 | loop fusion | flops 3670016 | bytes 9441280 | tf_op jit(solution)/shard_map/convert_element_type | solution.py:42
  172.8 0.0 copy-start.3
  172.8 3.7 %collective-permute-start.2 = (bf16[512,1024]{1,0:T(8,128)(2,1)}, bf16[512,1024]{1,0:T(8,128)(2,1)S(1)}, u32[]{:S(2)}, u32[]{:S(2)}) collective-permute-start(bf16[512,1024]{1,0:T(8,128)(2,1)} %get-tuple-element.13), channel_id=1, source_target_pairs={{0,16},{1,17},{2,18},{3,19},{4,20},{5,21},{6,22},{7,23},{8,24},{9,... | collective-permute-start | bytes 3145736 | tf_op jit(solution)/shard_map/ppermute | solution.py:42
  176.5 3.1 %fusion.9 = f32[1,5,64,1024]{3,2,1,0:T(8,128)} fusion(bf16[5,64,1024]{2,1,0:T(8,128)(2,1)} %get-tuple-element.9, f32[1,5,64,1024]{3,2,1,0:T(8,128)} %param.13, bf16[5,64,1024]{2,1,0:T(8,128)(2,1)} %get-tuple-element.10, pred[]{:T(512)S(6)} %eq.3), kind=kLoop, calls=%fused_computation.24 | loop fusion | flops 2949120 | bytes 3932161 | tf_op jit(solution)/shard_map/broadcast_in_dim | solution.py:451
  179.7 0.0 copy-done.3
  179.7 6.1 %fusion.1 = f32[1,1024,1024]{2,1,0:T(8,128)} fusion(bf16[1024,1024]{1,0:T(8,128)(2,1)} %get-tuple-element.7, f32[1,1024,1024]{2,1,0:T(8,128)} %param.12, bf16[1024,1024]{1,0:T(8,128)(2,1)S(1)} %copy-done.3, pred[]{:T(512)S(6)} %eq.3), kind=kLoop, calls=%fused_computation.4 | loop fusion | flops 9437184 | bytes 12582913 | tf_op jit(solution)/shard_map/broadcast_in_dim | solution.py:451
  185.8 0.0 copy-start.2
  185.8 13.3 %collective-permute-done.2 = bf16[512,1024]{1,0:T(8,128)(2,1)S(1)} collective-permute-done((bf16[512,1024]{1,0:T(8,128)(2,1)}, bf16[512,1024]{1,0:T(8,128)(2,1)S(1)}, u32[]{:S(2)}, u32[]{:S(2)}) %collective-permute-start.2) | collective-permute-done | bytes 1048608 | tf_op jit(solution)/shard_map/ppermute | solution.py:42
  199.1 2.8 %gather_fusion = bf16[512,1024]{1,0:T(8,128)(2,1)} fusion(bf16[512,1024]{1,0:T(8,128)(2,1)S(1)} %collective-permute-done.2, s32[1024]{0:T(1024)S(1)} %pad_clamp_fusion), kind=kCustom, calls=%fused_computation | custom fusion | bytes 2099200 | tf_op jit(solution)/shard_map/jit(_take)/gather | solution.py:449
  201.9 0.0 copy-done.2
  201.9 2.8 %select_bitcast_fusion = f32[1,512,1024]{2,1,0:T(8,128)} fusion(f32[512,1024]{1,0:T(8,128)S(1)} %copy-done.2, bf16[512,1024]{1,0:T(8,128)(2,1)} %gather_fusion, pred[512]{0:T(512)(128)(4,1)S(1)} %compare_and_fusion, pred[]{:T(512)S(6)} %eq.3), kind=kLoop, calls=%fused_computation.19 | loop fusion | flops 1572864 | bytes 5243393 | tf_op jit(solution)/shard_map/broadcast_in_dim | solution.py:451
  (3 shorter events, 0.0 us)
Async XLA Ops:
  0.6 9.8 %copy-start.1 = (f32[1,1024,1024]{2,1,0:T(8,128)S(1)}, f32[1,1024,1024]{2,1,0:T(8,128)}, u32[]{:S(2)}) copy-start(f32[1,1024,1024]{2,1,0:T(8,128)} %param.12) | copy-start | bytes 12582916
  2.7 166.8 %collective-permute-start = (f32[513,1]{1,0:T(8,128)}, f32[513,1]{1,0:T(8,128)S(1)}, u32[]{:S(2)}, u32[]{:S(2)}) collective-permute-start(f32[513,1]{1,0:T(8,128)} %get-tuple-element.15), channel_id=1, source_target_pairs={{0,1},{1,2},{2,3},{3,4},{4,5},{5,6},{6,7},{7,8},{8,9},{9,10},{10,1... | collective-permute-start | bytes 6164 | tf_op jit(solution)/shard_map/ppermute | solution.py:20
  3.2 166.5 %collective-permute-start.1 = (f32[513,1]{1,0:T(8,128)S(1)}, f32[513,1]{1,0:T(8,128)S(1)}, u32[]{:S(2)}, u32[]{:S(2)}) collective-permute-start(f32[513,1]{1,0:T(8,128)S(1)} %get-tuple-element.16), channel_id=1, source_target_pairs={{1,0},{2,1},{3,2},{4,3},{5,4},{6,5},{7,6},{8,7},{9,8},{10,9},{11,1... | collective-permute-start | bytes 6164 | tf_op jit(solution)/shard_map/ppermute | solution.py:21
  12.1 157.5 %copy-start.5 = (s32[512]{0:T(512)S(1)}, s32[512]{0:T(512)}, u32[]{:S(2)}) copy-start(s32[512]{0:T(512)} %param.11) | copy-start | bytes 6148
  12.1 157.5 %copy-start = (f32[1,512,1024]{2,1,0:T(8,128)S(1)}, f32[1,512,1024]{2,1,0:T(8,128)}, u32[]{:S(2)}) copy-start(f32[1,512,1024]{2,1,0:T(8,128)} %param.7) | copy-start | bytes 6291460
  12.1 157.5 %copy-start.4 = (f32[1024]{0:T(1024)S(1)}, f32[1024]{0:T(1024)}, u32[]{:S(2)}) copy-start(f32[1024]{0:T(1024)} %param.8) | copy-start | bytes 12292
  169.7 0.7 copy-start.6
  172.8 6.9 %copy-start.3 = (bf16[1024,1024]{1,0:T(8,128)(2,1)S(1)}, bf16[1024,1024]{1,0:T(8,128)(2,1)}, u32[]{:S(2)}) copy-start(bf16[1024,1024]{1,0:T(8,128)(2,1)} %get-tuple-element.8) | copy-start | bytes 6291460
  172.8 26.3 %collective-permute-start.2 = (bf16[512,1024]{1,0:T(8,128)(2,1)}, bf16[512,1024]{1,0:T(8,128)(2,1)S(1)}, u32[]{:S(2)}, u32[]{:S(2)}) collective-permute-start(bf16[512,1024]{1,0:T(8,128)(2,1)} %get-tuple-element.13), channel_id=1, source_target_pairs={{0,16},{1,17},{2,18},{3,19},{4,20},{5,21},{6,22},{7,23},{8,24},{9,... | collective-permute-start | bytes 3145736 | tf_op jit(solution)/shard_map/ppermute | solution.py:42
  185.8 16.1 %copy-start.2 = (f32[512,1024]{1,0:T(8,128)S(1)}, f32[512,1024]{1,0:T(8,128)}, u32[]{:S(2)}) copy-start(f32[512,1024]{1,0:T(8,128)} %get-tuple-element.14) | copy-start | bytes 6291460

commit v3 on v2

--- a/solution.py
+++ b/solution.py
@@ -46,7 +46,7 @@
     return lax.ppermute(value.astype(jnp.bfloat16), "role", [(1, 0)])
 
 
-def plain_training(features, hidden_narrow, out_narrow, own_fields, own_out, own_hidden):
+def plain_training(features, hidden_narrow, out_narrow, own_fields, own_out, own_hidden, fields):
     layer_count, unit_rows = own_hidden.shape[:2]
     batch = own_fields.shape[0]
     first_unit = lax.axis_index("tile") * unit_rows
@@ -84,7 +84,7 @@
     solver_side = lax.axis_index("role") == 0
     other_out = jnp.where(solver_side, sent_out, momentum_out)
     other_hidden = jnp.where(solver_side, jnp.stack(sent[::-1]), momentum_hidden)
-    return grad_out, jnp.stack(gradients[::-1]), other_out, other_hidden
+    return grad_out, jnp.stack(gradients[::-1]), other_out, other_hidden, to_trainer(fields)
 
 
 LANES = 128
@@ -93,14 +93,19 @@
 
 def train_kernel(
     groups,
-    features_ref,
+    features_hbm,
     hidden_ref,
-    out_ref,
-    target_ref,
+    out_hbm,
+    target_hbm,
+    fields_hbm,
     sent_out_ref,
     sent_hidden_ref,
     got_out_ref,
     got_hidden_ref,
+    got_fields_ref,
+    features_ref,
+    out_ref,
+    target_ref,
     weights,
     inputs,
     factors,
@@ -111,10 +116,16 @@
     payload_hidden,
     gradient,
     core_sum,
+    x_away,
     x_sum,
+    z_away,
     z_sum,
-    gather_send,
-    gather_recv,
+    z_send,
+    z_recv,
+    x_send,
+    x_recv,
+    core_send,
+    core_recv,
     sum_send,
     sum_recv,
     slope_send,
@@ -124,7 +135,7 @@
     local_sem,
 ):
     layer_count, unit_rows, width = hidden_ref.shape
-    batch = features_ref.shape[0]
+    batch, cells = target_ref.shape
     rows = partial.shape[3]
     role = lax.axis_index("role")
     tile = lax.axis_index("tile")
@@ -137,10 +148,12 @@
         return (role, z_at * 4 + x_at * 2 + core_at)
 
     z_places = [lax.rem(z + k, groups) for k in range(1, groups)]
+    z_origins = [lax.rem(z + groups - k, groups) for k in range(1, groups)]
     z_peers = [device(place, x, core) for place in z_places]
     x_peer = device(z, 1 - x, core)
     core_peer = device(z, x, 1 - core)
     role_peer = (1 - role, tile)
+    sends = []
 
     def send(source, target, send_sem, recv_sem, peer):
         copy = pltpu.make_async_remote_copy(
@@ -152,17 +165,37 @@
             device_id_type=pl.DeviceIdType.MESH,
         )
         copy.start()
+        sends.append(copy)
         return copy
 
     own = pltpu.make_async_copy(hidden_ref, weights.at[:, z, x, core], local_sem.at[0])
     own.start()
+    loads = [
+        pltpu.make_async_copy(features_hbm, features_ref, local_sem.at[1]),
+        pltpu.make_async_copy(out_hbm, out_ref, local_sem.at[2]),
+        pltpu.make_async_copy(target_hbm, target_ref, local_sem.at[3]),
+    ]
+    for load in loads:
+        load.start()
     barrier = pltpu.get_barrier_semaphore()
     peers = z_peers + [x_peer, core_peer, role_peer]
     for peer in peers:
         pl.semaphore_signal(barrier, inc=1, device_id=peer, device_id_type=pl.DeviceIdType.MESH)
     pl.semaphore_wait(barrier, len(peers))
 
-    sends = []
+    x_copies = [[] for _ in range(layer_count)]
+
+    def send_x(i, slot, source, place):
+        x_copies[i].append(
+            send(
+                source,
+                weights.at[i, place, x, core],
+                x_send.at[i, slot],
+                x_recv.at[i, slot],
+                x_peer,
+            )
+        )
+
     z_copies = []
     for i in range(layer_count):
         z_copies.append(
@@ -170,15 +203,26 @@
                 send(
                     hidden_ref.at[i],
                     weights.at[i, z, x, core],
-                    gather_send.at[i, k],
-                    gather_recv.at[i, k],
+                    z_send.at[i, k],
+                    z_recv.at[i, k],
                     z_peers[k],
                 )
                 for k in range(groups - 1)
             ]
         )
-        sends += z_copies[-1]
+        if i < 2:
+            send_x(i, 0, hidden_ref.at[i], z)
+    last = layer_count - 1
+    fields_copy = send(
+        fields_hbm,
+        got_fields_ref,
+        role_send.at[0],
+        role_recv.at[0],
+        role_peer,
+    )
     own.wait()
+    for load in loads:
+        load.wait()
 
     def columns_of(j):
         return pl.ds(pl.multiple_of(j * COLUMNS, COLUMNS), COLUMNS)
@@ -194,43 +238,55 @@
             inputs[i, :, columns] = (summed * logistic).astype(jnp.bfloat16)
             factors[i, :, columns] = logistic * (1.0 + summed * (1.0 - logistic))
 
-    x_copies, core_copies = [], []
+    core_copies = []
     for i in range(layer_count + 2):
         if i < layer_count:
-            for copy in z_copies[i]:
+            for k in range(groups - 1):
+                z_copies[i][k].wait_recv()
+                send_x(i, k + 1, weights.at[i, z_origins[k], x, core], z_origins[k])
+            if i + 2 < layer_count:
+                send_x(i + 2, 0, hidden_ref.at[i + 2], z)
+        if 1 <= i <= layer_count:
+            for copy in x_copies[i - 1]:
                 copy.wait_recv()
-            view = weights.at[i, :, x, core]
-            x_copies.append(
-                send(view, view, gather_send.at[i, groups - 1], gather_recv.at[i, groups - 1], x_peer)
-            )
-        if 1 <= i <= layer_count:
-            x_copies[i - 1].wait_recv()
             view = weights.at[i - 1, :, :, core]
             core_copies.append(
-                send(
-                    view,
-                    view,
-                    gather_send.at[i - 1, groups],
-                    gather_recv.at[i - 1, groups],
-                    core_peer,
-                )
+                send(view, view, core_send.at[i - 1], core_recv.at[i - 1], core_peer)
             )
         if i >= 2:
             core_copies[i - 2].wait_recv()
             forward(i - 2)
-    sends += x_copies + core_copies
-
-    last = layer_count - 1
-
-    @pl.loop(0, width // COLUMNS)
-    def _(j):
-        columns = columns_of(j)
+
+    role_slot = 1
+    chunks = [pl.ds(j * COLUMNS, COLUMNS) for j in range(cells // COLUMNS)]
+    role_copies = [fields_copy]
+    for columns in chunks:
         predicted = jnp.dot(inputs[last], out_ref[:, columns], preferred_element_type=jnp.float32)
         residual[:, columns] = ((predicted - target_ref[:, columns]) / batch).astype(jnp.bfloat16)
-
-    @pl.loop(0, width // COLUMNS)
-    def _(j):
-        columns = columns_of(j)
+    for columns in chunks:
+        grad = lax.dot_general(
+            inputs[last],
+            residual[:, columns],
+            (((0,), (0,)), ((), ())),
+            preferred_element_type=jnp.float32,
+        )
+        payload[:, columns] = jnp.where(solver_side, out_ref[:, columns], grad.astype(jnp.bfloat16))
+        role_copies.append(
+            send(
+                payload.at[:, columns],
+                got_out_ref.at[:, columns],
+                role_send.at[role_slot],
+                role_recv.at[role_slot],
+                role_peer,
+            )
+        )
+        role_slot += 1
+    out_keep = pltpu.make_async_copy(payload, sent_out_ref, local_sem.at[0])
+    out_keep.start()
+
+    parts = [pl.ds(j * COLUMNS, COLUMNS) for j in range(width // COLUMNS)]
+    core_sums, x_sums, z_sums, z_slopes, x_slopes, core_slopes = [], [], [], [], [], []
+    for j, columns in enumerate(parts):
         part = lax.dot_general(
             residual[...],
             out_ref[columns, :],
@@ -238,68 +294,79 @@
             preferred_element_type=jnp.float32,
         )
         partial[:, :, :, :, columns] = part.reshape(groups, 2, 2, rows, COLUMNS)
-
-    core_copy = send(
-        partial.at[:, :, 1 - core], core_sum, sum_send.at[0], sum_recv.at[0], core_peer
-    )
-
-    @pl.loop(0, width // COLUMNS)
-    def _(j):
-        columns = columns_of(j)
-        grad = lax.dot_general(
-            inputs[last],
-            residual[:, columns],
-            (((0,), (0,)), ((), ())),
-            preferred_element_type=jnp.float32,
-        )
-        payload[:, columns] = jnp.where(solver_side, out_ref[:, columns], grad.astype(jnp.bfloat16))
-
-    core_copy.wait_recv()
-    away = partial[:, 1 - x, core] + core_sum[:, 1 - x]
-    partial[:, 1 - x, core] = away
-    x_copy = send(partial.at[:, 1 - x, core], x_sum, sum_send.at[1], sum_recv.at[1], x_peer)
-    out_copy = send(payload, got_out_ref, role_send.at[0], role_recv.at[0], role_peer)
-    out_keep = pltpu.make_async_copy(payload, sent_out_ref, local_sem.at[0])
-    out_keep.start()
-    partial[:, x, core] = partial[:, x, core] + core_sum[:, x]
-    x_copy.wait_recv()
-    partial[:, x, core] = partial[:, x, core] + x_sum[...]
-    z_sums = [
-        send(
-            partial.at[z_places[k], x, core],
-            z_sum.at[k],
-            sum_send.at[2 + k],
-            sum_recv.at[2 + k],
-            z_peers[k],
-        )
-        for k in range(groups - 1)
-    ]
-    upstream = partial[z, x, core]
-    for k in range(groups - 1):
-        z_sums[k].wait_recv()
-        upstream = upstream + z_sum[k]
+        core_sums.append(
+            send(
+                partial.at[:, :, 1 - core, :, columns],
+                core_sum.at[:, :, :, columns],
+                sum_send.at[j, 0],
+                sum_recv.at[j, 0],
+                core_peer,
+            )
+        )
+    for j, columns in enumerate(parts):
+        core_sums[j].wait_recv()
+        away = partial[:, 1 - x, core, :, columns] + core_sum[:, 1 - x, :, columns]
+        x_away[:, :, columns] = away.astype(jnp.bfloat16)
+        x_sums.append(
+            send(
+                x_away.at[:, :, columns],
+                x_sum.at[:, :, columns],
+                sum_send.at[j, 1],
+                sum_recv.at[j, 1],
+                x_peer,
+            )
+        )
+    for j, columns in enumerate(parts):
+        kept = partial[:, x, core, :, columns] + core_sum[:, x, :, columns]
+        x_sums[j].wait_recv()
+        kept = kept + x_sum[:, :, columns].astype(jnp.float32)
+        partial[:, x, core, :, columns] = kept
+        z_away[:, :, columns] = kept.astype(jnp.bfloat16)
+        z_sums.append(
+            [
+                send(
+                    z_away.at[z_places[k], :, columns],
+                    z_sum.at[k, :, columns],
+                    sum_send.at[j, 2 + k],
+                    sum_recv.at[j, 2 + k],
+                    z_peers[k],
+                )
+                for k in range(groups - 1)
+            ]
+        )
     own_rows = pl.ds(pl.multiple_of(tile * rows, rows), rows)
-    slope[z, x, core] = (upstream * factors[last, own_rows, :]).astype(jnp.bfloat16)
-    view = slope.at[z, x, core]
-    z_slopes = [
-        send(view, view, slope_send.at[k], slope_recv.at[k], z_peers[k]) for k in range(groups - 1)
-    ]
-    for copy in z_slopes:
+
+    def send_slope(view, j, slot, peer):
+        return send(view, view, slope_send.at[j, slot], slope_recv.at[j, slot], peer)
+
+    for j, columns in enumerate(parts):
+        upstream = partial[z, x, core, :, columns]
+        for k in range(groups - 1):
+            z_sums[j][k].wait_recv()
+            upstream = upstream + z_sum[k, :, columns].astype(jnp.float32)
+        slope[z, x, core, :, columns] = (upstream * factors[last, own_rows, columns]).astype(
+            jnp.bfloat16
+        )
+        view = slope.at[z, x, core, :, columns]
+        z_slopes.append([send_slope(view, j, k, z_peers[k]) for k in range(groups - 1)])
+    for j, columns in enumerate(parts):
+        for copy in z_slopes[j]:
+            copy.wait_recv()
+        view = slope.at[:, x, core, :, columns]
+        x_slopes.append(send_slope(view, j, groups - 1, x_peer))
+    for j, columns in enumerate(parts):
+        x_slopes[j].wait_recv()
+        core_slopes.append(send_slope(slope.at[:, :, core, :, columns], j, groups, core_peer))
+    for copy in core_slopes:
         copy.wait_recv()
-    view = slope.at[:, x, core]
-    x_slope = send(view, view, slope_send.at[groups - 1], slope_recv.at[groups - 1], x_peer)
-    x_slope.wait_recv()
-    view = slope.at[:, :, core]
-    core_slope = send(view, view, slope_send.at[groups], slope_recv.at[groups], core_peer)
-    core_slope.wait_recv()
-    sends += [core_copy, x_copy, out_copy] + z_sums
-    for copy in z_slopes + [x_slope, core_slope]:
-        copy.wait_send()
+    for copies in z_slopes + [x_slopes, core_slopes]:
+        for copy in copies:
+            copy.wait_send()
+            sends[:] = [other for other in sends if other is not copy]
 
     per_block = LANES // unit_rows
     first_lane = pl.multiple_of((tile // per_block) * LANES, LANES)
     unit_first = pl.multiple_of(lax.rem(tile, per_block) * unit_rows, unit_rows)
-    role_copies = []
     for i in reversed(range(layer_count)):
         source = features_ref if i == 0 else inputs.at[i - 1]
         own_inputs = source[:, pl.ds(first_lane, LANES)]
@@ -335,17 +402,16 @@
             send(
                 payload_hidden.at[i],
                 got_hidden_ref.at[i],
-                role_send.at[1 + i],
-                role_recv.at[1 + i],
+                role_send.at[role_slot],
+                role_recv.at[role_slot],
                 role_peer,
             )
         )
+        role_slot += 1
         if i > 0:
             slope[...] = residual[...].reshape(slope.shape)
     hidden_keep = pltpu.make_async_copy(payload_hidden, sent_hidden_ref, local_sem.at[1])
     hidden_keep.start()
-    sends += role_copies
-    out_copy.wait_recv()
     for copy in role_copies:
         copy.wait_recv()
     for copy in sends:
@@ -354,7 +420,7 @@
     hidden_keep.wait()
 
 
-def fused_training(features, hidden_narrow, out_narrow, own_fields, own_out, own_hidden):
+def fused_training(features, hidden_narrow, out_narrow, own_fields, own_out, own_hidden, fields):
     layer_count, unit_rows, width = hidden_narrow.shape
     batch, cells = own_fields.shape
     groups = lax.axis_size("tile") // 4
@@ -363,6 +429,8 @@
     dma = pltpu.SemaphoreType.DMA
     vmem = pl.BlockSpec(memory_space=pltpu.VMEM)
     anywhere = pl.BlockSpec(memory_space=pl.ANY)
+    parts = width // COLUMNS
+    role_slots = 1 + cells // COLUMNS + layer_count
     return pl.pallas_call(
         functools.partial(train_kernel, groups),
         out_shape=(
@@ -370,10 +438,14 @@
             jax.ShapeDtypeStruct(hidden_narrow.shape, narrow),
             jax.ShapeDtypeStruct((width, cells), narrow),
             jax.ShapeDtypeStruct(hidden_narrow.shape, narrow),
+            jax.ShapeDtypeStruct((batch, cells), narrow),
         ),
-        in_specs=[vmem] * 4,
-        out_specs=[anywhere] * 4,
+        in_specs=[anywhere, vmem] + [anywhere] * 3,
+        out_specs=[anywhere] * 5,
         scratch_shapes=[
+            pltpu.VMEM((batch, width), narrow),
+            pltpu.VMEM((width, cells), narrow),
+            pltpu.VMEM((batch, cells), wide),
             pltpu.VMEM((layer_count, groups, 2, 2, unit_rows, width), narrow),
             pltpu.VMEM((layer_count, batch, width), narrow),
             pltpu.VMEM((layer_count, batch, width), wide),
@@ -384,17 +456,23 @@
             pltpu.VMEM(hidden_narrow.shape, narrow),
             pltpu.VMEM((LANES, width), wide),
             pltpu.VMEM((groups, 2, rows, width), wide),
-            pltpu.VMEM((groups, rows, width), wide),
-            pltpu.VMEM((groups - 1, rows, width), wide),
-            dma((layer_count, groups + 1)),
-            dma((layer_count, groups + 1)),
-            dma((groups + 1,)),
-            dma((groups + 1,)),
-            dma((groups + 1,)),
-            dma((groups + 1,)),
-            dma((layer_count + 1,)),
-            dma((layer_count + 1,)),
-            dma((2,)),
+            pltpu.VMEM((groups, rows, width), narrow),
+            pltpu.VMEM((groups, rows, width), narrow),
+            pltpu.VMEM((groups, rows, width), narrow),
+            pltpu.VMEM((groups - 1, rows, width), narrow),
+            dma((layer_count, groups - 1)),
+            dma((layer_count, groups - 1)),
+            dma((layer_count, groups)),
+            dma((layer_count, groups)),
+            dma((layer_count,)),
+            dma((layer_count,)),
+            dma((parts, groups + 1)),
+            dma((parts, groups + 1)),
+            dma((parts, groups + 1)),
+            dma((parts, groups + 1)),
+            dma((role_slots,)),
+            dma((role_slots,)),
+            dma((4,)),
         ],
         compiler_params=pltpu.CompilerParams(
             collective_id=0, has_side_effects=True, vmem_limit_bytes=64000000
@@ -402,10 +480,10 @@
         cost_estimate=pl.CostEstimate(
             flops=60 * batch * width * width, bytes_accessed=40 * batch * width, transcendentals=0
         ),
-    )(features, hidden_narrow, out_narrow, own_fields)
-
-
-def training(features, hidden_narrow, out_narrow, own_fields, own_out, own_hidden):
+    )(features, hidden_narrow, out_narrow, own_fields, fields)
+
+
+def training(features, hidden_narrow, out_narrow, own_fields, own_out, own_hidden, fields):
     tiles = lax.axis_size("tile")
     fits = (
         tiles % 4 == 0
@@ -414,7 +492,7 @@
         and LANES % own_hidden.shape[1] == 0
     )
     chosen = fused_training if fits else plain_training
-    return chosen(features, hidden_narrow, out_narrow, own_fields, own_out, own_hidden)
+    return chosen(features, hidden_narrow, out_narrow, own_fields, own_out, own_hidden, fields)
 
 
 def body(fields_pair, velocity, growth, features, assignment, out_pair, hidden_pair):
@@ -424,14 +502,14 @@
     own_hidden = hidden_pair[0]
     stacked = jnp.concatenate([own_fields, velocity[None, :]], axis=0)
     advanced = advance(extended(stacked, "tile", 1, 1), growth)
-    fresh_fields = to_trainer(advanced)
-    grad_out, grad_hidden, other_out, other_hidden = training(
+    grad_out, grad_hidden, other_out, other_hidden, fresh_fields = training(
         features,
         own_hidden.astype(jnp.bfloat16),
         own_out.astype(jnp.bfloat16),
         own_fields,
         own_out,
         own_hidden,
+        advanced.astype(jnp.bfloat16),
     )
     grad_out, grad_hidden, other_out, other_hidden = (
         v.astype(jnp.float32) for v in (grad_out, grad_hidden, other_out, other_hidden)

time: 205 us -> 175 us (0.85)
  Pallas kernels: 157 us -> 142 us
  waiting for transfers between devices: 13.3 us -> 4.56 us
  starting transfers between devices: 9.16 us -> 5.5 us
  other arithmetic: 21.3 us -> 17.9 us
  local copies, waits for them, and re-layouts: 2.8 us -> 4.87 us
    pallas_call x1, Pallas kernels: 157 us -> 142 us  [fused_training(): pl.pallas_call(functools.partial(train_kernel, groups), out_shape=(jax.Sh...]
    ppermute x1 -> x0, waiting for transfers between devices: 13.3 us -> none  [to_trainer(): return lax.ppermute(value.astype(jnp.bfloat16), 'role', [(0, 1)])]
    ppermute x1, waiting for transfers between devices: 0.01 us -> 4.55 us  [extended(): before = lax.ppermute(last, axis, up)]
    ppermute x1 -> x0, starting transfers between devices: 3.72 us -> none  [to_trainer(): return lax.ppermute(value.astype(jnp.bfloat16), 'role', [(0, 1)])]
    broadcast_in_dim x3, other arithmetic: 12.1 us -> 9.37 us  [body(): return (fields_next[None], out_next[None], hidden_next[None])]
  transfers between devices with their start and end apart: 3 -> 2, of which waited for: 1 -> 1; matrix products, arithmetic and copies ran while one was open for 6% -> 2% of each run, Pallas kernels for 77% -> 0%
where the time goes in v3:
time: 175 us
  Pallas kernels  142 us (81%)
  other arithmetic  17.9 us (10%)
  starting transfers between devices  5.5 us (3%)
  local copies, waits for them, and re-layouts  4.87 us (3%)
  waiting for transfers between devices  4.56 us (3%)
    pallas_call x1, Pallas kernels, fused_training(): pl.pallas_call(functools.partial(train_kernel, groups), out_shape=(jax.Sh...  142 us
    broadcast_in_dim x3, other arithmetic, body(): return (fields_next[None], out_next[None], hidden_next[None])  9.37 us
    ppermute x1, starting transfers between devices, extended(): after = lax.ppermute(leading, axis, down)  5.5 us
    ppermute x1, waiting for transfers between devices, extended(): before = lax.ppermute(last, axis, up)  4.55 us
    gather x1, local copies, waits for them, and re-layouts, body(): next_batch = jnp.take(fresh_fields, assignment, axis=0).astype(jnp.float32)  4.24 us
  transfers between devices with their start and end apart: 2, of which 1 were waited for; matrix products, arithmetic and copies ran while one was open for 2% of the time, Pallas kernels for 0%

profile of v3, /device:TPU:0, one launch (start us, length us, event | category | flops | bytes accessed | tf_op | source)
XLA Modules:
  0.0 175.1 jit_solution(4313661101380759744)
XLA Ops:
  0.6 0.0 copy-start.8
  0.6 0.0 copy-start.1
  0.7 1.3 pad_maximum_fusion.5
  2.0 5.5 %collective-permute-start.1 = (f32[513,1]{1,0:T(8,128)S(1)}, f32[513,1]{1,0:T(8,128)S(1)}, u32[]{:S(2)}, u32[]{:S(2)}) collective-permute-start(f32[513,1]{1,0:T(8,128)S(1)} %get-tuple-element.18), channel_id=1, source_target_pairs={{1,0},{2,1},{3,2},{4,3},{5,4},{6,5},{7,6},{8,7},{9,8},{10,9},{11,1... | collective-permute-start | bytes 6164 | tf_op jit(solution)/shard_map/ppermute | solution.py:21
  7.5 0.0 collective-permute-start
  7.5 0.0 copy-done.8
  7.5 2.3 %bitcast_convert_fusion.1.hidden_ref = bf16[5,64,1024]{2,1,0:T(8,128)(2,1)} fusion(f32[1,5,64,1024]{3,2,1,0:T(8,128)} %param.13), kind=kLoop, calls=%fused_computation.29 | loop fusion | flops 327680 | bytes 1966080 | tf_op jit(solution)/shard_map/convert_element_type | solution.py:507
  9.8 0.0 copy-done.1
  9.8 1.6 bitcast_convert_fusion.out_hbm
  11.5 4.6 %collective-permute-done = f32[513,1]{1,0:T(8,128)S(1)} collective-permute-done((f32[513,1]{1,0:T(8,128)S(1)}, f32[513,1]{1,0:T(8,128)S(1)}, u32[]{:S(2)}, u32[]{:S(2)}) %collective-permute-start) | collective-permute-done | bytes 2084 | tf_op jit(solution)/shard_map/ppermute | solution.py:20
  16.0 0.0 copy-done
  16.0 0.0 copy-done.7
  16.0 0.1 maximum_reduce_fusion
  16.2 0.0 collective-permute-done.1
  16.2 0.0 copy-start.9
  16.2 0.7 fusion.6
  16.9 0.0 copy-done.9
  16.9 2.4 %fusion.13 = (bf16[512,1024]{1,0:T(8,128)(2,1)}, f32[512,1024]{1,0:T(8,128)}) fusion(f32[1024]{0:T(1024)S(1)} %copy-done.9, f32[512,1025]{1,0:T(8,128)S(1)} %fusion.6, f32[1,512,1024]{2,1,0:T(8,128)S(1)} %copy-done), kind=kLoop, calls=%fused_computation.38 | loop fusion | flops 3670016 | bytes 9441280 | tf_op jit(solution)/shard_map/convert_element_type | solution.py:512
  19.3 141.6 %shard_map.94 = (bf16[1024,1024]{1,0:T(8,128)(2,1)}, bf16[5,64,1024]{2,1,0:T(8,128)(2,1)}, bf16[1024,1024]{1,0:T(8,128)(2,1)}, bf16[5,64,1024]{2,1,0:T(8,128)(2,1)}, bf16[512,1024]{1,0:T(8,128)(2,1)}) custom-call(bf16[512,1024]{1,0:T(8,128)(2,1)} %features_hbm.1, bf16[5,64,1024]{2,1,0:T(8,128)(2,1)} %bitcast_convert_fusion.1.hidden_ref, ...), custom_call_target="tpu_custom_call" | custom-call | flops 32212254720 | bytes 20971520 | tf_op jit(solution)/shard_map/pallas_call | solution.py:434
  160.9 0.0 copy-start.4
  160.9 4.2 %gather_fusion = bf16[512,1024]{1,0:T(8,128)(2,1)S(1)} fusion(bf16[512,1024]{1,0:T(8,128)(2,1)} %get-tuple-element.8, s32[1024]{0:T(1024)S(1)} %pad_clamp_fusion), kind=kCustom, calls=%fused_computation | custom fusion | bytes 2099200 | tf_op jit(solution)/shard_map/jit(_take)/gather | solution.py:527
  165.1 0.0 copy-done.4
  165.1 0.0 copy-start.3
  165.1 0.0 copy-start.5
  165.1 0.0 copy-start.6
  165.1 6.3 %fusion.1 = f32[1,1024,1024]{2,1,0:T(8,128)} fusion(bf16[1024,1024]{1,0:T(8,128)(2,1)} %get-tuple-element.9, f32[1,1024,1024]{2,1,0:T(8,128)} %param.12, bf16[1024,1024]{1,0:T(8,128)(2,1)S(1)} %copy-done.4, pred[]{:T(512)S(6)} %eq.3), kind=kLoop, calls=%fused_computation.4 | loop fusion | flops 9437184 | bytes 12582913 | tf_op jit(solution)/shard_map/broadcast_in_dim | solution.py:529
  171.4 0.0 copy-done.3
  171.4 0.0 copy-done.5
  171.4 0.0 copy-done.6
  171.5 1.5 fusion.9
  172.9 0.6 copy-done.2
  173.5 1.6 select_bitcast_fusion
  (6 shorter events, 0.0 us)
Async XLA Ops:
  0.6 6.9 %copy-start.8 = (s32[512]{0:T(512)S(1)}, s32[512]{0:T(512)}, u32[]{:S(2)}) copy-start(s32[512]{0:T(512)} %param.11) | copy-start | bytes 6148
  0.6 9.2 %copy-start.1 = (f32[1,1024,1024]{2,1,0:T(8,128)S(1)}, f32[1,1024,1024]{2,1,0:T(8,128)}, u32[]{:S(2)}) copy-start(f32[1,1024,1024]{2,1,0:T(8,128)} %param.12) | copy-start | bytes 12582916
  2.0 14.1 %collective-permute-start.1 = (f32[513,1]{1,0:T(8,128)S(1)}, f32[513,1]{1,0:T(8,128)S(1)}, u32[]{:S(2)}, u32[]{:S(2)}) collective-permute-start(f32[513,1]{1,0:T(8,128)S(1)} %get-tuple-element.18), channel_id=1, source_target_pairs={{1,0},{2,1},{3,2},{4,3},{5,4},{6,5},{7,6},{8,7},{9,8},{10,9},{11,1... | collective-permute-start | bytes 6164 | tf_op jit(solution)/shard_map/ppermute | solution.py:21
  7.5 8.5 %collective-permute-start = (f32[513,1]{1,0:T(8,128)S(1)}, f32[513,1]{1,0:T(8,128)S(1)}, u32[]{:S(2)}, u32[]{:S(2)}) collective-permute-start(f32[513,1]{1,0:T(8,128)S(1)} %get-tuple-element.17), channel_id=1, source_target_pairs={{0,1},{1,2},{2,3},{3,4},{4,5},{5,6},{6,7},{7,8},{8,9},{9,10},{10,1... | collective-permute-start | bytes 6164 | tf_op jit(solution)/shard_map/ppermute | solution.py:20
  9.8 6.2 %copy-start = (f32[1,512,1024]{2,1,0:T(8,128)S(1)}, f32[1,512,1024]{2,1,0:T(8,128)}, u32[]{:S(2)}) copy-start(f32[1,512,1024]{2,1,0:T(8,128)} %param.7) | copy-start | bytes 6291460
  9.8 6.2 %copy-start.7 = (f32[1024]{0:T(1024)S(1)}, f32[1024]{0:T(1024)}, u32[]{:S(2)}) copy-start(f32[1024]{0:T(1024)} %param.8) | copy-start | bytes 12292
  16.2 0.7 copy-start.9
  160.9 4.3 %copy-start.4 = (bf16[1024,1024]{1,0:T(8,128)(2,1)S(1)}, bf16[1024,1024]{1,0:T(8,128)(2,1)}, u32[]{:S(2)}) copy-start(bf16[1024,1024]{1,0:T(8,128)(2,1)} %get-tuple-element.10) | copy-start | bytes 6291460
  165.1 6.3 %copy-start.3 = (f32[1,5,64,1024]{3,2,1,0:T(8,128)S(1)}, f32[1,5,64,1024]{3,2,1,0:T(8,128)}, u32[]{:S(2)}) copy-start(f32[1,5,64,1024]{3,2,1,0:T(8,128)} %param.13) | copy-start | bytes 3932164
  165.1 6.3 %copy-start.5 = (bf16[5,64,1024]{2,1,0:T(8,128)(2,1)S(1)}, bf16[5,64,1024]{2,1,0:T(8,128)(2,1)}, u32[]{:S(2)}) copy-start(bf16[5,64,1024]{2,1,0:T(8,128)(2,1)} %get-tuple-element.12) | copy-start | bytes 1966084
  165.1 6.3 %copy-start.6 = (bf16[5,64,1024]{2,1,0:T(8,128)(2,1)S(1)}, bf16[5,64,1024]{2,1,0:T(8,128)(2,1)}, u32[]{:S(2)}) copy-start(bf16[5,64,1024]{2,1,0:T(8,128)(2,1)} %get-tuple-element.11) | copy-start | bytes 1966084
  171.4 2.1 %copy-start.2 = (f32[512,1024]{1,0:T(8,128)S(1)}, f32[512,1024]{1,0:T(8,128)}, u32[]{:S(2)}) copy-start(f32[512,1024]{1,0:T(8,128)} %get-tuple-element.16) | copy-start | bytes 6291460

commit v4 on v3

--- a/solution.py
+++ b/solution.py
@@ -82,9 +82,9 @@
                 slope, full_hidden[i], (((1,), (1,)), ((), ())), preferred_element_type=jnp.float32
             )
     solver_side = lax.axis_index("role") == 0
-    other_out = jnp.where(solver_side, sent_out, momentum_out)
+    grad_out = jnp.where(solver_side, sent_out.astype(jnp.float32), grad_out)
     other_hidden = jnp.where(solver_side, jnp.stack(sent[::-1]), momentum_hidden)
-    return grad_out, jnp.stack(gradients[::-1]), other_out, other_hidden, to_trainer(fields)
+    return grad_out, jnp.stack(gradients[::-1]), momentum_out, other_hidden, to_trainer(fields)
 
 
 LANES = 128
@@ -98,7 +98,7 @@
     out_hbm,
     target_hbm,
     fields_hbm,
-    sent_out_ref,
+    grad_out_ref,
     sent_hidden_ref,
     got_out_ref,
     got_hidden_ref,
@@ -110,6 +110,9 @@
     inputs,
     factors,
     residual,
+    next_slope,
+    got_residual,
+    got_inputs,
     partial,
     slope,
     payload,
@@ -213,13 +216,16 @@
         if i < 2:
             send_x(i, 0, hidden_ref.at[i], z)
     last = layer_count - 1
-    fields_copy = send(
-        fields_hbm,
-        got_fields_ref,
-        role_send.at[0],
-        role_recv.at[0],
-        role_peer,
-    )
+    role_copies = []
+
+    def send_role(source, target):
+        slot = len(role_copies)
+        copy = send(source, target, role_send.at[slot], role_recv.at[slot], role_peer)
+        role_copies.append(copy)
+        return copy
+
+    send_role(fields_hbm, got_fields_ref)
+    send_role(out_hbm, got_out_ref)
     own.wait()
     for load in loads:
         load.wait()
@@ -238,51 +244,48 @@
             inputs[i, :, columns] = (summed * logistic).astype(jnp.bfloat16)
             factors[i, :, columns] = logistic * (1.0 + summed * (1.0 - logistic))
 
-    core_copies = []
+    core_copies = [[] for _ in range(layer_count)]
+
+    def send_core(i, place, x_at, source=None):
+        slot = len(core_copies[i])
+        view = weights.at[i, place, x_at, core]
+        core_copies[i].append(
+            send(
+                view if source is None else source,
+                view,
+                core_send.at[i, slot],
+                core_recv.at[i, slot],
+                core_peer,
+            )
+        )
+
+    for i in range(layer_count):
+        send_core(i, z, x, hidden_ref.at[i])
     for i in range(layer_count + 2):
         if i < layer_count:
             for k in range(groups - 1):
                 z_copies[i][k].wait_recv()
                 send_x(i, k + 1, weights.at[i, z_origins[k], x, core], z_origins[k])
+                send_core(i, z_origins[k], x)
             if i + 2 < layer_count:
                 send_x(i + 2, 0, hidden_ref.at[i + 2], z)
         if 1 <= i <= layer_count:
-            for copy in x_copies[i - 1]:
+            for slot, place in enumerate([z] + z_origins):
+                x_copies[i - 1][slot].wait_recv()
+                send_core(i - 1, place, 1 - x)
+        if i >= 2:
+            for copy in core_copies[i - 2]:
                 copy.wait_recv()
-            view = weights.at[i - 1, :, :, core]
-            core_copies.append(
-                send(view, view, core_send.at[i - 1], core_recv.at[i - 1], core_peer)
-            )
-        if i >= 2:
-            core_copies[i - 2].wait_recv()
             forward(i - 2)
 
-    role_slot = 1
+    half = batch // 2
+    half_rows = pl.ds(pl.multiple_of(core * half, half), half)
+    inputs_copy = send_role(inputs.at[last, half_rows, :], got_inputs.at[half_rows, :])
     chunks = [pl.ds(j * COLUMNS, COLUMNS) for j in range(cells // COLUMNS)]
-    role_copies = [fields_copy]
     for columns in chunks:
         predicted = jnp.dot(inputs[last], out_ref[:, columns], preferred_element_type=jnp.float32)
         residual[:, columns] = ((predicted - target_ref[:, columns]) / batch).astype(jnp.bfloat16)
-    for columns in chunks:
-        grad = lax.dot_general(
-            inputs[last],
-            residual[:, columns],
-            (((0,), (0,)), ((), ())),
-            preferred_element_type=jnp.float32,
-        )
-        payload[:, columns] = jnp.where(solver_side, out_ref[:, columns], grad.astype(jnp.bfloat16))
-        role_copies.append(
-            send(
-                payload.at[:, columns],
-                got_out_ref.at[:, columns],
-                role_send.at[role_slot],
-                role_recv.at[role_slot],
-                role_peer,
-            )
-        )
-        role_slot += 1
-    out_keep = pltpu.make_async_copy(payload, sent_out_ref, local_sem.at[0])
-    out_keep.start()
+        send_role(residual.at[:, columns], got_residual.at[:, columns])
 
     parts = [pl.ds(j * COLUMNS, COLUMNS) for j in range(width // COLUMNS)]
     core_sums, x_sums, z_sums, z_slopes, x_slopes, core_slopes = [], [], [], [], [], []
@@ -364,6 +367,10 @@
             copy.wait_send()
             sends[:] = [other for other in sends if other is not copy]
 
+    inputs_copy.wait_recv()
+    view = got_inputs.at[half_rows, :]
+    inputs_swap = send(view, view, local_sem.at[0], local_sem.at[2], core_peer)
+
     per_block = LANES // unit_rows
     first_lane = pl.multiple_of((tile // per_block) * LANES, LANES)
     unit_first = pl.multiple_of(lax.rem(tile, per_block) * unit_rows, unit_rows)
@@ -396,28 +403,36 @@
                     (((1,), (1,)), ((), ())),
                     preferred_element_type=jnp.float32,
                 )
-                residual[:, columns] = (back * factors[i - 1, :, columns]).astype(jnp.bfloat16)
-
-        role_copies.append(
-            send(
-                payload_hidden.at[i],
-                got_hidden_ref.at[i],
-                role_send.at[role_slot],
-                role_recv.at[role_slot],
-                role_peer,
-            )
-        )
-        role_slot += 1
+                next_slope[:, columns] = (back * factors[i - 1, :, columns]).astype(jnp.bfloat16)
+
+        send_role(payload_hidden.at[i], got_hidden_ref.at[i])
         if i > 0:
-            slope[...] = residual[...].reshape(slope.shape)
+            slope[...] = next_slope[...].reshape(slope.shape)
     hidden_keep = pltpu.make_async_copy(payload_hidden, sent_hidden_ref, local_sem.at[1])
     hidden_keep.start()
+    inputs_swap.wait_recv()
     for copy in role_copies:
-        copy.wait_recv()
+        if copy is not inputs_copy:
+            copy.wait_recv()
+    chosen = jnp.where(solver_side, got_inputs[...], inputs[last])
+    keeps = [hidden_keep]
+    for j, columns in enumerate(chunks):
+        grad = lax.dot_general(
+            chosen,
+            jnp.where(solver_side, got_residual[:, columns], residual[:, columns]),
+            (((0,), (0,)), ((), ())),
+            preferred_element_type=jnp.float32,
+        )
+        payload[:, columns] = grad.astype(jnp.bfloat16)
+        keep = pltpu.make_async_copy(
+            payload.at[:, columns], grad_out_ref.at[:, columns], local_sem.at[4 + j]
+        )
+        keep.start()
+        keeps.append(keep)
     for copy in sends:
         copy.wait_send()
-    out_keep.wait()
-    hidden_keep.wait()
+    for keep in keeps:
+        keep.wait()
 
 
 def fused_training(features, hidden_narrow, out_narrow, own_fields, own_out, own_hidden, fields):
@@ -430,7 +445,7 @@
     vmem = pl.BlockSpec(memory_space=pltpu.VMEM)
     anywhere = pl.BlockSpec(memory_space=pl.ANY)
     parts = width // COLUMNS
-    role_slots = 1 + cells // COLUMNS + layer_count
+    role_slots = 3 + cells // COLUMNS + layer_count
     return pl.pallas_call(
         functools.partial(train_kernel, groups),
         out_shape=(
@@ -450,6 +465,9 @@
             pltpu.VMEM((layer_count, batch, width), narrow),
             pltpu.VMEM((layer_count, batch, width), wide),
             pltpu.VMEM((batch, cells), narrow),
+            pltpu.VMEM((batch, width), narrow),
+            pltpu.VMEM((batch, cells), narrow),
+            pltpu.VMEM((batch, width), narrow),
             pltpu.VMEM((groups, 2, 2, rows, width), wide),
             pltpu.VMEM((groups, 2, 2, rows, width), narrow),
             pltpu.VMEM((width, cells), narrow),
@@ -464,15 +482,15 @@
             dma((layer_count, groups - 1)),
             dma((layer_count, groups)),
             dma((layer_count, groups)),
-            dma((layer_count,)),
-            dma((layer_count,)),
+            dma((layer_count, 2 * groups)),
+            dma((layer_count, 2 * groups)),
             dma((parts, groups + 1)),
             dma((parts, groups + 1)),
             dma((parts, groups + 1)),
             dma((parts, groups + 1)),
             dma((role_slots,)),
             dma((role_slots,)),
-            dma((4,)),
+            dma((4 + cells // COLUMNS,)),
         ],
         compiler_params=pltpu.CompilerParams(
             collective_id=0, has_side_effects=True, vmem_limit_bytes=64000000
@@ -516,7 +534,7 @@
     )
     out_next = jnp.where(
         solver_side,
-        momentum_decay * own_out + other_out,
+        momentum_decay * own_out + grad_out,
         own_out - step_size * (momentum_decay * other_out + grad_out),
     )
     hidden_next = jnp.where(

time: 175 us -> 164 us (0.937)
  Pallas kernels: 142 us -> 130 us
    pallas_call x1, Pallas kernels: 142 us -> 130 us  [fused_training(): pl.pallas_call(functools.partial(train_kernel, groups), out_shape=(jax.Sh...]
where the time goes in v4:
time: 164 us
  Pallas kernels  130 us (79%)
  other arithmetic  17.9 us (11%)
  starting transfers between devices  5.5 us (3%)
  local copies, waits for them, and re-layouts  4.87 us (3%)
  waiting for transfers between devices  4.56 us (3%)
    pallas_call x1, Pallas kernels, fused_training(): pl.pallas_call(functools.partial(train_kernel, groups), out_shape=(jax.Sh...  130 us
    broadcast_in_dim x3, other arithmetic, body(): return (fields_next[None], out_next[None], hidden_next[None])  9.4 us
    ppermute x1, starting transfers between devices, extended(): after = lax.ppermute(leading, axis, down)  5.5 us
    ppermute x1, waiting for transfers between devices, extended(): before = lax.ppermute(last, axis, up)  4.55 us
    gather x1, local copies, waits for them, and re-layouts, body(): next_batch = jnp.take(fresh_fields, assignment, axis=0).astype(jnp.float32)  4.24 us
  transfers between devices with their start and end apart: 2, of which 1 were waited for; matrix products, arithmetic and copies ran while one was open for 2% of the time, Pallas kernels for 0%

profile of v4, /device:TPU:0, one launch (start us, length us, event | category | flops | bytes accessed | tf_op | source)
XLA Modules:
  0.0 164.0 jit_solution(12847702135590524586)
XLA Ops:
  0.6 0.0 copy-start.8
  0.6 0.0 copy-start.1
  0.7 1.3 pad_maximum_fusion.5
  2.0 5.5 %collective-permute-start.1 = (f32[513,1]{1,0:T(8,128)S(1)}, f32[513,1]{1,0:T(8,128)S(1)}, u32[]{:S(2)}, u32[]{:S(2)}) collective-permute-start(f32[513,1]{1,0:T(8,128)S(1)} %get-tuple-element.18), channel_id=1, source_target_pairs={{1,0},{2,1},{3,2},{4,3},{5,4},{6,5},{7,6},{8,7},{9,8},{10,9},{11,1... | collective-permute-start | bytes 6164 | tf_op jit(solution)/shard_map/ppermute | solution.py:21
  7.5 0.0 collective-permute-start
  7.5 0.0 copy-done.8
  7.5 2.3 %bitcast_convert_fusion.1.hidden_ref = bf16[5,64,1024]{2,1,0:T(8,128)(2,1)} fusion(f32[1,5,64,1024]{3,2,1,0:T(8,128)} %param.13), kind=kLoop, calls=%fused_computation.28 | loop fusion | flops 327680 | bytes 1966080 | tf_op jit(solution)/shard_map/convert_element_type | solution.py:525
  9.8 0.0 copy-done.1
  9.8 1.6 %bitcast_convert_fusion.out_hbm = bf16[1024,1024]{1,0:T(8,128)(2,1)} fusion(f32[1,1024,1024]{2,1,0:T(8,128)S(1)} %copy-done.1), kind=kLoop, calls=%fused_computation.8 | loop fusion | flops 1048576 | bytes 6291456 | tf_op jit(solution)/shard_map/convert_element_type | solution.py:526
  11.5 4.6 %collective-permute-done = f32[513,1]{1,0:T(8,128)S(1)} collective-permute-done((f32[513,1]{1,0:T(8,128)S(1)}, f32[513,1]{1,0:T(8,128)S(1)}, u32[]{:S(2)}, u32[]{:S(2)}) %collective-permute-start) | collective-permute-done | bytes 2084 | tf_op jit(solution)/shard_map/ppermute | solution.py:20
  16.0 0.0 copy-done
  16.0 0.0 copy-done.7
  16.0 0.1 maximum_reduce_fusion
  16.2 0.0 collective-permute-done.1
  16.2 0.0 copy-start.9
  16.2 0.7 fusion.5
  16.9 0.0 copy-done.9
  16.9 2.4 %fusion.12 = (bf16[512,1024]{1,0:T(8,128)(2,1)}, f32[512,1024]{1,0:T(8,128)}) fusion(f32[1024]{0:T(1024)S(1)} %copy-done.9, f32[512,1025]{1,0:T(8,128)S(1)} %fusion.5, f32[1,512,1024]{2,1,0:T(8,128)S(1)} %copy-done), kind=kLoop, calls=%fused_computation.37 | loop fusion | flops 3670016 | bytes 9441280 | tf_op jit(solution)/shard_map/convert_element_type | solution.py:530
  19.3 130.4 %shard_map.94 = (bf16[1024,1024]{1,0:T(8,128)(2,1)}, bf16[5,64,1024]{2,1,0:T(8,128)(2,1)}, bf16[1024,1024]{1,0:T(8,128)(2,1)}, bf16[5,64,1024]{2,1,0:T(8,128)(2,1)}, bf16[512,1024]{1,0:T(8,128)(2,1)}) custom-call(bf16[512,1024]{1,0:T(8,128)(2,1)} %features_hbm.1, bf16[5,64,1024]{2,1,0:T(8,128)(2,1)} %bitcast_convert_fusion.1.hidden_ref, ...), custom_call_target="tpu_custom_call" | custom-call | flops 32212254720 | bytes 20971520 | tf_op jit(solution)/shard_map/pallas_call | solution.py:449
  149.6 0.0 copy-start.4
  149.7 4.2 %gather_fusion = bf16[512,1024]{1,0:T(8,128)(2,1)S(1)} fusion(bf16[512,1024]{1,0:T(8,128)(2,1)} %get-tuple-element.8, s32[1024]{0:T(1024)S(1)} %pad_clamp_fusion), kind=kCustom, calls=%fused_computation | custom fusion | bytes 2099200 | tf_op jit(solution)/shard_map/jit(_take)/gather | solution.py:545
  153.9 0.0 copy-done.4
  153.9 0.0 copy-start.3
  153.9 0.0 copy-start.5
  153.9 0.0 copy-start.6
  153.9 6.3 %fusion.1 = f32[1,1024,1024]{2,1,0:T(8,128)} fusion(bf16[1024,1024]{1,0:T(8,128)(2,1)S(1)} %copy-done.4, f32[1,1024,1024]{2,1,0:T(8,128)} %param.12, bf16[1024,1024]{1,0:T(8,128)(2,1)} %get-tuple-element.10, pred[]{:T(512)S(6)} %eq.3), kind=kLoop, calls=%fused_computation.4 | loop fusion | flops 9437184 | bytes 12582913 | tf_op jit(solution)/shard_map/broadcast_in_dim | solution.py:547
  160.3 0.0 copy-done.3
  160.3 0.0 copy-done.5
  160.3 0.0 copy-done.6
  160.3 1.5 fusion.8
  161.7 0.6 copy-done.2
  162.3 1.6 select_bitcast_fusion
  (6 shorter events, 0.0 us)
Async XLA Ops:
  0.6 6.9 %copy-start.8 = (s32[512]{0:T(512)S(1)}, s32[512]{0:T(512)}, u32[]{:S(2)}) copy-start(s32[512]{0:T(512)} %param.11) | copy-start | bytes 6148
  0.6 9.2 %copy-start.1 = (f32[1,1024,1024]{2,1,0:T(8,128)S(1)}, f32[1,1024,1024]{2,1,0:T(8,128)}, u32[]{:S(2)}) copy-start(f32[1,1024,1024]{2,1,0:T(8,128)} %param.12) | copy-start | bytes 12582916
  2.0 14.1 %collective-permute-start.1 = (f32[513,1]{1,0:T(8,128)S(1)}, f32[513,1]{1,0:T(8,128)S(1)}, u32[]{:S(2)}, u32[]{:S(2)}) collective-permute-start(f32[513,1]{1,0:T(8,128)S(1)} %get-tuple-element.18), channel_id=1, source_target_pairs={{1,0},{2,1},{3,2},{4,3},{5,4},{6,5},{7,6},{8,7},{9,8},{10,9},{11,1... | collective-permute-start | bytes 6164 | tf_op jit(solution)/shard_map/ppermute | solution.py:21
  7.5 8.5 %collective-permute-start = (f32[513,1]{1,0:T(8,128)S(1)}, f32[513,1]{1,0:T(8,128)S(1)}, u32[]{:S(2)}, u32[]{:S(2)}) collective-permute-start(f32[513,1]{1,0:T(8,128)S(1)} %get-tuple-element.17), channel_id=1, source_target_pairs={{0,1},{1,2},{2,3},{3,4},{4,5},{5,6},{6,7},{7,8},{8,9},{9,10},{10,1... | collective-permute-start | bytes 6164 | tf_op jit(solution)/shard_map/ppermute | solution.py:20
  9.8 6.2 %copy-start = (f32[1,512,1024]{2,1,0:T(8,128)S(1)}, f32[1,512,1024]{2,1,0:T(8,128)}, u32[]{:S(2)}) copy-start(f32[1,512,1024]{2,1,0:T(8,128)} %param.7) | copy-start | bytes 6291460
  9.8 6.2 %copy-start.7 = (f32[1024]{0:T(1024)S(1)}, f32[1024]{0:T(1024)}, u32[]{:S(2)}) copy-start(f32[1024]{0:T(1024)} %param.8) | copy-start | bytes 12292
  16.2 0.7 copy-start.9
  149.6 4.3 %copy-start.4 = (bf16[1024,1024]{1,0:T(8,128)(2,1)S(1)}, bf16[1024,1024]{1,0:T(8,128)(2,1)}, u32[]{:S(2)}) copy-start(bf16[1024,1024]{1,0:T(8,128)(2,1)} %get-tuple-element.9) | copy-start | bytes 6291460
  153.9 6.4 %copy-start.3 = (f32[1,5,64,1024]{3,2,1,0:T(8,128)S(1)}, f32[1,5,64,1024]{3,2,1,0:T(8,128)}, u32[]{:S(2)}) copy-start(f32[1,5,64,1024]{3,2,1,0:T(8,128)} %param.13) | copy-start | bytes 3932164
  153.9 6.3 %copy-start.5 = (bf16[5,64,1024]{2,1,0:T(8,128)(2,1)S(1)}, bf16[5,64,1024]{2,1,0:T(8,128)(2,1)}, u32[]{:S(2)}) copy-start(bf16[5,64,1024]{2,1,0:T(8,128)(2,1)} %get-tuple-element.12) | copy-start | bytes 1966084
  153.9 6.3 %copy-start.6 = (bf16[5,64,1024]{2,1,0:T(8,128)(2,1)S(1)}, bf16[5,64,1024]{2,1,0:T(8,128)(2,1)}, u32[]{:S(2)}) copy-start(bf16[5,64,1024]{2,1,0:T(8,128)(2,1)} %get-tuple-element.11) | copy-start | bytes 1966084
  160.3 2.1 %copy-start.2 = (f32[512,1024]{1,0:T(8,128)S(1)}, f32[512,1024]{1,0:T(8,128)}, u32[]{:S(2)}) copy-start(f32[512,1024]{1,0:T(8,128)} %get-tuple-element.16) | copy-start | bytes 6291460

commit v5 on v4

--- a/solution.py
+++ b/solution.py
@@ -213,7 +213,7 @@
                 for k in range(groups - 1)
             ]
         )
-        if i < 2:
+        if i < 3:
             send_x(i, 0, hidden_ref.at[i], z)
     last = layer_count - 1
     role_copies = []
@@ -267,8 +267,8 @@
                 z_copies[i][k].wait_recv()
                 send_x(i, k + 1, weights.at[i, z_origins[k], x, core], z_origins[k])
                 send_core(i, z_origins[k], x)
-            if i + 2 < layer_count:
-                send_x(i + 2, 0, hidden_ref.at[i + 2], z)
+            if i + 3 < layer_count:
+                send_x(i + 3, 0, hidden_ref.at[i + 3], z)
         if 1 <= i <= layer_count:
             for slot, place in enumerate([z] + z_origins):
                 x_copies[i - 1][slot].wait_recv()
@@ -282,10 +282,11 @@
     half_rows = pl.ds(pl.multiple_of(core * half, half), half)
     inputs_copy = send_role(inputs.at[last, half_rows, :], got_inputs.at[half_rows, :])
     chunks = [pl.ds(j * COLUMNS, COLUMNS) for j in range(cells // COLUMNS)]
+    residual_copies = []
     for columns in chunks:
         predicted = jnp.dot(inputs[last], out_ref[:, columns], preferred_element_type=jnp.float32)
         residual[:, columns] = ((predicted - target_ref[:, columns]) / batch).astype(jnp.bfloat16)
-        send_role(residual.at[:, columns], got_residual.at[:, columns])
+        residual_copies.append(send_role(residual.at[:, columns], got_residual.at[:, columns]))
 
     parts = [pl.ds(j * COLUMNS, COLUMNS) for j in range(width // COLUMNS)]
     core_sums, x_sums, z_sums, z_slopes, x_slopes, core_slopes = [], [], [], [], [], []
@@ -411,9 +412,8 @@
     hidden_keep = pltpu.make_async_copy(payload_hidden, sent_hidden_ref, local_sem.at[1])
     hidden_keep.start()
     inputs_swap.wait_recv()
-    for copy in role_copies:
-        if copy is not inputs_copy:
-            copy.wait_recv()
+    for copy in residual_copies:
+        copy.wait_recv()
     chosen = jnp.where(solver_side, got_inputs[...], inputs[last])
     keeps = [hidden_keep]
     for j, columns in enumerate(chunks):
@@ -429,6 +429,10 @@
         )
         keep.start()
         keeps.append(keep)
+    waited = [inputs_copy] + residual_copies
+    for copy in role_copies:
+        if not any(copy is other for other in waited):
+            copy.wait_recv()
     for copy in sends:
         copy.wait_send()
     for keep in keeps:

time: 164 us -> 159 us (0.970)
  Pallas kernels: 130 us -> 125 us
    pallas_call x1, Pallas kernels: 130 us -> 125 us  [fused_training(): pl.pallas_call(functools.partial(train_kernel, groups), out_shape=(jax.Sh...]
  transfers between devices with their start and end apart: 2 -> 2, of which waited for: 1 -> 1; matrix products, arithmetic and copies ran while one was open for 2% -> 3% of each run, Pallas kernels for 0% -> 0%
where the time goes in v5:
time: 159 us
  Pallas kernels  125 us (79%)
  other arithmetic  17.9 us (11%)
  starting transfers between devices  5.5 us (3%)
  local copies, waits for them, and re-layouts  4.87 us (3%)
  waiting for transfers between devices  4.56 us (3%)
    pallas_call x1, Pallas kernels, fused_training(): pl.pallas_call(functools.partial(train_kernel, groups), out_shape=(jax.Sh...  125 us
    broadcast_in_dim x3, other arithmetic, body(): return (fields_next[None], out_next[None], hidden_next[None])  9.4 us
    ppermute x1, starting transfers between devices, extended(): after = lax.ppermute(leading, axis, down)  5.5 us
    ppermute x1, waiting for transfers between devices, extended(): before = lax.ppermute(last, axis, up)  4.55 us
    gather x1, local copies, waits for them, and re-layouts, body(): next_batch = jnp.take(fresh_fields, assignment, axis=0).astype(jnp.float32)  4.24 us
  transfers between devices with their start and end apart: 2, of which 1 were waited for; matrix products, arithmetic and copies ran while one was open for 3% of the time, Pallas kernels for 0%

profile of v5, /device:TPU:0, one launch (start us, length us, event | category | flops | bytes accessed | tf_op | source)
XLA Modules:
  0.0 158.8 jit_solution(14964906275522872902)
XLA Ops:
  0.6 0.0 copy-start.8
  0.6 0.0 copy-start.1
  0.7 1.3 pad_maximum_fusion.5
  2.0 5.5 %collective-permute-start.1 = (f32[513,1]{1,0:T(8,128)S(1)}, f32[513,1]{1,0:T(8,128)S(1)}, u32[]{:S(2)}, u32[]{:S(2)}) collective-permute-start(f32[513,1]{1,0:T(8,128)S(1)} %get-tuple-element.18), channel_id=1, source_target_pairs={{1,0},{2,1},{3,2},{4,3},{5,4},{6,5},{7,6},{8,7},{9,8},{10,9},{11,1... | collective-permute-start | bytes 6164 | tf_op jit(solution)/shard_map/ppermute | solution.py:21
  7.5 0.0 collective-permute-start
  7.5 0.0 copy-done.8
  7.5 2.3 %bitcast_convert_fusion.1.hidden_ref = bf16[5,64,1024]{2,1,0:T(8,128)(2,1)} fusion(f32[1,5,64,1024]{3,2,1,0:T(8,128)} %param.13), kind=kLoop, calls=%fused_computation.28 | loop fusion | flops 327680 | bytes 1966080 | tf_op jit(solution)/shard_map/convert_element_type | solution.py:529
  9.8 0.0 copy-done.1
  9.8 1.6 %bitcast_convert_fusion.out_hbm = bf16[1024,1024]{1,0:T(8,128)(2,1)} fusion(f32[1,1024,1024]{2,1,0:T(8,128)S(1)} %copy-done.1), kind=kLoop, calls=%fused_computation.8 | loop fusion | flops 1048576 | bytes 6291456 | tf_op jit(solution)/shard_map/convert_element_type | solution.py:530
  11.5 4.6 %collective-permute-done = f32[513,1]{1,0:T(8,128)S(1)} collective-permute-done((f32[513,1]{1,0:T(8,128)S(1)}, f32[513,1]{1,0:T(8,128)S(1)}, u32[]{:S(2)}, u32[]{:S(2)}) %collective-permute-start) | collective-permute-done | bytes 2084 | tf_op jit(solution)/shard_map/ppermute | solution.py:20
  16.0 0.0 copy-done
  16.0 0.0 copy-done.7
  16.0 0.1 maximum_reduce_fusion
  16.2 0.0 collective-permute-done.1
  16.2 0.0 copy-start.9
  16.2 0.7 fusion.5
  16.9 0.0 copy-done.9
  16.9 2.4 %fusion.12 = (bf16[512,1024]{1,0:T(8,128)(2,1)}, f32[512,1024]{1,0:T(8,128)}) fusion(f32[1024]{0:T(1024)S(1)} %copy-done.9, f32[512,1025]{1,0:T(8,128)S(1)} %fusion.5, f32[1,512,1024]{2,1,0:T(8,128)S(1)} %copy-done), kind=kLoop, calls=%fused_computation.37 | loop fusion | flops 3670016 | bytes 9441280 | tf_op jit(solution)/shard_map/convert_element_type | solution.py:534
  19.3 125.2 %shard_map.94 = (bf16[1024,1024]{1,0:T(8,128)(2,1)}, bf16[5,64,1024]{2,1,0:T(8,128)(2,1)}, bf16[1024,1024]{1,0:T(8,128)(2,1)}, bf16[5,64,1024]{2,1,0:T(8,128)(2,1)}, bf16[512,1024]{1,0:T(8,128)(2,1)}) custom-call(bf16[512,1024]{1,0:T(8,128)(2,1)} %features_hbm.1, bf16[5,64,1024]{2,1,0:T(8,128)(2,1)} %bitcast_convert_fusion.1.hidden_ref, ...), custom_call_target="tpu_custom_call" | custom-call | flops 32212254720 | bytes 20971520 | tf_op jit(solution)/shard_map/pallas_call | solution.py:453
  144.5 0.0 copy-start.4
  144.5 4.2 %gather_fusion = bf16[512,1024]{1,0:T(8,128)(2,1)S(1)} fusion(bf16[512,1024]{1,0:T(8,128)(2,1)} %get-tuple-element.8, s32[1024]{0:T(1024)S(1)} %pad_clamp_fusion), kind=kCustom, calls=%fused_computation | custom fusion | bytes 2099200 | tf_op jit(solution)/shard_map/jit(_take)/gather | solution.py:549
  148.8 0.0 copy-done.4
  148.8 0.0 copy-start.3
  148.8 0.0 copy-start.5
  148.8 0.0 copy-start.6
  148.8 6.3 %fusion.1 = f32[1,1024,1024]{2,1,0:T(8,128)} fusion(bf16[1024,1024]{1,0:T(8,128)(2,1)S(1)} %copy-done.4, f32[1,1024,1024]{2,1,0:T(8,128)} %param.12, bf16[1024,1024]{1,0:T(8,128)(2,1)} %get-tuple-element.10, pred[]{:T(512)S(6)} %eq.3), kind=kLoop, calls=%fused_computation.4 | loop fusion | flops 9437184 | bytes 12582913 | tf_op jit(solution)/shard_map/broadcast_in_dim | solution.py:551
  155.2 0.0 copy-done.3
  155.2 0.0 copy-done.5
  155.2 0.0 copy-done.6
  155.2 1.5 fusion.8
  156.6 0.6 copy-done.2
  157.2 1.6 %select_bitcast_fusion = f32[1,512,1024]{2,1,0:T(8,128)} fusion(f32[512,1024]{1,0:T(8,128)S(1)} %copy-done.2, bf16[512,1024]{1,0:T(8,128)(2,1)S(1)} %gather_fusion, pred[512]{0:T(512)(128)(4,1)S(1)} %compare_and_fusion, pred[]{:T(512)S(6)} %eq.3), kind=kLoop, calls=%fused_computation.18 | loop fusion | flops 1572864 | bytes 5243393 | tf_op jit(solution)/shard_map/broadcast_in_dim | solution.py:551
  (6 shorter events, 0.0 us)
Async XLA Ops:
  0.6 6.9 %copy-start.8 = (s32[512]{0:T(512)S(1)}, s32[512]{0:T(512)}, u32[]{:S(2)}) copy-start(s32[512]{0:T(512)} %param.11) | copy-start | bytes 6148
  0.6 9.2 %copy-start.1 = (f32[1,1024,1024]{2,1,0:T(8,128)S(1)}, f32[1,1024,1024]{2,1,0:T(8,128)}, u32[]{:S(2)}) copy-start(f32[1,1024,1024]{2,1,0:T(8,128)} %param.12) | copy-start | bytes 12582916
  2.0 14.1 %collective-permute-start.1 = (f32[513,1]{1,0:T(8,128)S(1)}, f32[513,1]{1,0:T(8,128)S(1)}, u32[]{:S(2)}, u32[]{:S(2)}) collective-permute-start(f32[513,1]{1,0:T(8,128)S(1)} %get-tuple-element.18), channel_id=1, source_target_pairs={{1,0},{2,1},{3,2},{4,3},{5,4},{6,5},{7,6},{8,7},{9,8},{10,9},{11,1... | collective-permute-start | bytes 6164 | tf_op jit(solution)/shard_map/ppermute | solution.py:21
  7.5 8.5 %collective-permute-start = (f32[513,1]{1,0:T(8,128)S(1)}, f32[513,1]{1,0:T(8,128)S(1)}, u32[]{:S(2)}, u32[]{:S(2)}) collective-permute-start(f32[513,1]{1,0:T(8,128)S(1)} %get-tuple-element.17), channel_id=1, source_target_pairs={{0,1},{1,2},{2,3},{3,4},{4,5},{5,6},{6,7},{7,8},{8,9},{9,10},{10,1... | collective-permute-start | bytes 6164 | tf_op jit(solution)/shard_map/ppermute | solution.py:20
  9.8 6.2 %copy-start = (f32[1,512,1024]{2,1,0:T(8,128)S(1)}, f32[1,512,1024]{2,1,0:T(8,128)}, u32[]{:S(2)}) copy-start(f32[1,512,1024]{2,1,0:T(8,128)} %param.7) | copy-start | bytes 6291460
  9.8 6.2 %copy-start.7 = (f32[1024]{0:T(1024)S(1)}, f32[1024]{0:T(1024)}, u32[]{:S(2)}) copy-start(f32[1024]{0:T(1024)} %param.8) | copy-start | bytes 12292
  16.2 0.7 copy-start.9
  144.5 4.3 %copy-start.4 = (bf16[1024,1024]{1,0:T(8,128)(2,1)S(1)}, bf16[1024,1024]{1,0:T(8,128)(2,1)}, u32[]{:S(2)}) copy-start(bf16[1024,1024]{1,0:T(8,128)(2,1)} %get-tuple-element.9) | copy-start | bytes 6291460
  148.8 6.4 %copy-start.3 = (f32[1,5,64,1024]{3,2,1,0:T(8,128)S(1)}, f32[1,5,64,1024]{3,2,1,0:T(8,128)}, u32[]{:S(2)}) copy-start(f32[1,5,64,1024]{3,2,1,0:T(8,128)} %param.13) | copy-start | bytes 3932164
  148.8 6.3 %copy-start.5 = (bf16[5,64,1024]{2,1,0:T(8,128)(2,1)S(1)}, bf16[5,64,1024]{2,1,0:T(8,128)(2,1)}, u32[]{:S(2)}) copy-start(bf16[5,64,1024]{2,1,0:T(8,128)(2,1)} %get-tuple-element.12) | copy-start | bytes 1966084
  148.8 6.3 %copy-start.6 = (bf16[5,64,1024]{2,1,0:T(8,128)(2,1)S(1)}, bf16[5,64,1024]{2,1,0:T(8,128)(2,1)}, u32[]{:S(2)}) copy-start(bf16[5,64,1024]{2,1,0:T(8,128)(2,1)} %get-tuple-element.11) | copy-start | bytes 1966084
  155.1 2.1 %copy-start.2 = (f32[512,1024]{1,0:T(8,128)S(1)}, f32[512,1024]{1,0:T(8,128)}, u32[]{:S(2)}) copy-start(f32[512,1024]{1,0:T(8,128)} %get-tuple-element.16) | copy-start | bytes 6291460
